TPU v7x, 32 devices: a whole 2x2x4 slice. The times are simulated.
32 devices in a mesh: groups: 2 (over x), patch: 16 (over z, y, core).
Axes of the slice: x: 2, y: 2, z: 4, core: 2. Of those that a mesh axis runs over, the one named last changes fastest.
Arguments:
- template: float32 [64, 32768], P(None, ('groups', 'patch')), parts along dimension 1, may hold values from -6 to 6
- science: float32 [512, 4, 128], P(('groups', 'patch')), parts along dimension 0, may hold values from -6 to 6
- dest: int32 [512, 1], P(('groups', 'patch')), parts along dimension 0, may hold values from 0 to 15; in each aligned block of 16 rows (0 to 15, 16 to 31, ...) at most 2 rows name the same one
- row_offset: int32 [512], P(('groups', 'patch')), parts along dimension 0, may hold values from 0 to 60
- col_block: int32 [512], P(('groups', 'patch')), parts along dimension 0, may hold values from 0 to 7
- basis_rows: float32 [27, 21], replicated, may hold values from -1.25 to 1.25
- basis_cols: float32 [27, 21], replicated, may hold values from -1.25 to 1.25
- stamp_rows: int32 [32, 24], P('groups'), parts along dimension 0, may hold values from 0 to 63
- stamp_cols: int32 [32, 24], P('groups'), parts along dimension 0, may hold values from 0 to 1023
Outputs:
- difference: float32 [512, 4, 128], P(('groups', 'patch')), parts along dimension 0
There are 2 independent parts, one for each index of `groups`. A program takes and returns all parts, laid end to end along the dimension named above; an argument that names none is the same for every part. Nothing has to cross between parts.
Inputs may be any that keep to these rules, and one draw needn't show every extreme that they name: `dest`: each visit sends at most 2 strips to one sub-patch, and in every draw some visit sends exactly 2 to one.
All inputs are finite; a program needn't handle non-finite values.
Results may differ from a plain program's by a relative error of at most 0.0003.
Values sent between devices are 32-bit elements; how exact they have to be, the bound alone decides.
No kernel may reach another device: no remote copies, remote signals or barrier semaphores. Data moves between devices by JAX's collectives and lax.ppermute only.
A program may use at most 64 MiB of HBM per device.

v0:
```python
import math

import jax
import jax.numpy as jnp
from jax import lax
from jax.sharding import PartitionSpec as P

CAP = 2
STAMP_HALF = 10


HIGH = lax.Precision.HIGHEST
RIDGE = 1.0


def with_halo(cells, sides, width):
    for axis, dim in sides:
        count = lax.axis_size(axis)
        ends = count - 1
        head = lax.slice_in_dim(cells, 0, width, axis=dim)
        tail = lax.slice_in_dim(cells, cells.shape[dim] - width, cells.shape[dim], axis=dim)
        cells = jnp.concatenate(
            [
                lax.ppermute(tail, axis, [(i, (i + 1) % count) for i in range(ends)]),
                cells,
                lax.ppermute(head, axis, [((i + 1) % count, i) for i in range(ends)]),
            ],
            axis=dim,
        )
    return cells


def filter_field(padded, row_taps, col_taps):
    taps = row_taps.shape[0]
    out_rows = padded.shape[0] - taps + 1
    out_cols = padded.shape[1] - taps + 1
    across = jnp.zeros((padded.shape[0], out_cols), jnp.float32)
    for shift_tap in range(taps):
        across = across + col_taps[shift_tap] * padded[:, shift_tap : shift_tap + out_cols]
    result = jnp.zeros((out_rows, out_cols), jnp.float32)
    for shift_tap in range(taps):
        result = result + row_taps[shift_tap] * across[shift_tap : shift_tap + out_rows, :]
    return result


def stamp_mask(row_start, blocks, stamp_r, stamp_c, strip_rows, block_cols):
    rows_here = row_start[:, None] + jnp.arange(strip_rows, dtype=jnp.int32)[None, :]
    cols_here = blocks[:, None] * block_cols + jnp.arange(block_cols, dtype=jnp.int32)[None, :]
    row_hit = (jnp.abs(rows_here[:, :, None] - stamp_r[:, None, :]) <= STAMP_HALF).astype(
        jnp.float32
    )
    col_hit = (jnp.abs(stamp_c[:, :, None] - cols_here[:, None, :]) <= STAMP_HALF).astype(
        jnp.float32
    )
    counts = jnp.einsum("nis,nsj->nij", row_hit, col_hit, precision=HIGH)
    return jnp.minimum(counts, 1.0)


def design_of(conv, info_rows, own_stamp_r, own_stamp_c, strip_rows, block_cols):
    row_start = info_rows[:, 0].astype(jnp.int32)
    blocks = info_rows[:, 1].astype(jnp.int32)
    live = info_rows[:, 2]

    def window_of(first_row, block):
        return lax.dynamic_slice(
            conv,
            (jnp.int32(0), first_row, block * block_cols),
            (conv.shape[0], strip_rows, block_cols),
        )

    windows = jax.vmap(window_of)(row_start, blocks)
    n_items = info_rows.shape[0]
    flattened = windows.reshape(n_items, windows.shape[1], -1)
    design = jnp.concatenate(
        [flattened, jnp.ones((n_items, 1, flattened.shape[2]), jnp.float32)], axis=1
    )
    stamp_r = jnp.broadcast_to(own_stamp_r[None, :], (n_items, own_stamp_r.shape[0]))
    stamp_c = jnp.broadcast_to(own_stamp_c[None, :], (n_items, own_stamp_c.shape[0]))
    weight = (
        stamp_mask(row_start, blocks, stamp_r, stamp_c, strip_rows, block_cols)
        * live[:, None, None]
    )
    weighted = design * weight.reshape(n_items, 1, -1)
    return (design, weighted)


def factor_of(design, weighted, capacity):
    n_items = design.shape[0]
    columns = design.shape[1]
    normal = jnp.einsum("skp,slp->skl", weighted, design, precision=HIGH)
    pair_normal = normal.reshape(n_items // capacity, capacity, columns, columns).sum(axis=1)
    pair_normal = pair_normal + RIDGE * jnp.eye(columns, dtype=jnp.float32)
    return jnp.linalg.cholesky(pair_normal)


def finish_fit(design, weighted, factor, pixels, capacity):
    n_items = design.shape[0]
    columns = design.shape[1]
    values = pixels.reshape(n_items, -1)
    moment = jnp.einsum("skp,sp->sk", weighted, values, precision=HIGH)
    pair_moment = moment.reshape(n_items // capacity, capacity, columns).sum(axis=1)
    inner = lax.linalg.triangular_solve(factor, pair_moment[..., None], left_side=True, lower=True)
    coefficients = lax.linalg.triangular_solve(
        factor, inner, left_side=True, lower=True, transpose_a=True
    )[..., 0]
    slot_coeff = jnp.repeat(coefficients, capacity, axis=0)
    model_image = jnp.einsum("skp,sk->sp", design, slot_coeff, precision=HIGH)
    return (values - model_image).reshape(pixels.shape)


def on_device(
    template, science, dest, row_offset, col_block, basis_rows, basis_cols, stamp_rows, stamp_cols
):
    peers = lax.axis_size("patch")
    own_index = lax.axis_index("patch")
    half_taps = (basis_rows.shape[1] - 1) // 2
    strips, strip_rows, block_cols = science.shape
    capacity = CAP
    slots = peers * capacity
    group_pairs = math.gcd(peers, 16)
    n_groups = peers // group_pairs
    per_group = group_pairs * capacity
    haloed = with_halo(template, (("patch", 1),), half_taps)
    framed = jnp.pad(haloed, ((half_taps, half_taps), (0, 0)))
    targets = dest[:, 0]
    strip_order = jnp.arange(strips, dtype=jnp.int32)
    earlier = (targets[:, None] == targets[None, :]) & (strip_order[None, :] < strip_order[:, None])
    rank_of = jnp.sum(earlier.astype(jnp.int32), axis=1)
    slot_of = targets * capacity + rank_of
    slot_ids = jnp.arange(slots, dtype=jnp.int32)
    slot_hot = (slot_ids[:, None] == slot_of[None, :]).astype(jnp.float32)
    strip_hot = (slot_of[:, None] == slot_ids[None, :]).astype(jnp.float32)
    positions = jnp.stack([row_offset, col_block, jnp.ones_like(row_offset)], axis=1).astype(
        jnp.float32
    )
    slot_info = jnp.dot(slot_hot, positions, precision=HIGH)
    outgoing = jnp.dot(slot_hot, science.reshape(strips, -1), precision=HIGH).reshape(
        slots, strip_rows, block_cols
    )
    own_stamp_r = lax.dynamic_index_in_dim(stamp_rows, own_index, 0, keepdims=False)
    own_stamp_c = lax.dynamic_index_in_dim(stamp_cols, own_index, 0, keepdims=False)
    arrived, arrived_info = (
        lax.all_to_all(outgoing, "patch", split_axis=0, concat_axis=0, tiled=True),
        lax.all_to_all(slot_info, "patch", split_axis=0, concat_axis=0, tiled=True),
    )

    def one_basis(row_taps, col_taps):
        return filter_field(framed, row_taps, col_taps)

    conv = jax.vmap(one_basis)(basis_rows, basis_cols)

    def fit_group(group):
        pixels, info_rows = group
        design, weighted = design_of(
            conv, info_rows, own_stamp_r, own_stamp_c, strip_rows, block_cols
        )
        factor = factor_of(design, weighted, capacity)
        return finish_fit(design, weighted, factor, pixels, capacity)

    grouped = lax.map(
        fit_group,
        (
            arrived.reshape(n_groups, per_group, strip_rows, block_cols),
            arrived_info.reshape(n_groups, per_group, 3),
        ),
    )
    residuals = grouped.reshape(slots, strip_rows, block_cols)
    returned = lax.all_to_all(residuals, "patch", split_axis=0, concat_axis=0, tiled=True)
    picked = jnp.dot(strip_hot, returned.reshape(slots, -1), precision=HIGH)
    return picked.reshape(strips, strip_rows, block_cols)


def solution(mesh):
    placed = (
        P(None, ("groups", "patch")),
        P(("groups", "patch"), None, None),
        P(("groups", "patch"), None),
        P(("groups", "patch")),
        P(("groups", "patch")),
        P(),
        P(),
        P("groups", None),
        P("groups", None),
    )
    return jax.shard_map(
        on_device,
        mesh=mesh,
        in_specs=placed,
        out_specs=P(("groups", "patch"), None, None),
        check_vma=False,
    )
```

profile of v0, /device:TPU:0, one launch (start us, length us, event | category | flops | bytes accessed | tf_op | source)
XLA Modules:
  0.0 338.4 jit_solution(11568813379290508286)
XLA Ops:
  7.7 9.3 %all-to-all-start.1 = ((f32[16,2,3]{2,1,0:T(2,128)}), f32[16,2,3]{2,1,0:T(2,128)S(1)}, u32[]{:S(2)}, u32[]{:S(2)}) async-start(f32[16,2,3]{2,1,0:T(2,128)} %bitcast.50), calls=%async_computation.1 | async-start | bytes 32768 | tf_op jit(solution)/shard_map/all_to_all | solution.py:144
  23.5 5.5 %all-to-all-start = ((f32[32,4,128]{2,1,0:T(4,128)}), f32[32,4,128]{2,1,0:T(4,128)S(1)}, u32[]{:S(2)}, u32[]{:S(2)}) async-start(f32[32,4,128]{2,1,0:T(4,128)} %copy.40), calls=%async_computation | async-start | bytes 131072 | tf_op jit(solution)/shard_map/all_to_all | solution.py:143
  33.0 19.8 %multiply_add_fusion = f32[27,84,1024]{2,1,0:T(8,128)} fusion(f32[84,1024]{1,0:T(8,128)S(1)} %get-tuple-element.64, f32[27]{0:T(128)S(1)} %get-tuple-element.111, f32[84,1024]{1,0:T(8,128)S(1)} %get-tuple-element.63, f32[27]{0:T(128)S(1)} %get-tuple-element.110, f32[84,1024]{1,0:T(8,128)S(1)} %get-tuple-element.62, f32[27]{0:T(128)S(1)} %get-tuple-element.92, ...), kind=kLoop, calls=%fused_computation.2 | loop fusion | flops 95219712 | bytes 16517340 | tf_op jit(solution)/shard_map/vmap()/add | solution.py:39
  52.7 73.2 %fusion = f32[27,64,1024]{2,1,0:T(8,128)} fusion(f32[27,84,1024]{2,1,0:T(8,128)} %multiply_add_fusion, f32[27]{0:T(128)S(1)} %get-tuple-element.90, f32[27]{0:T(128)S(1)} %get-tuple-element.89, f32[27]{0:T(128)S(1)} %get-tuple-element.71, f32[27]{0:T(128)S(1)} %get-tuple-element.72, f32[27]{0:T(128)S(1)} %get-tuple-element.73, f32[27]{0:T(128)S(1)} %get-tuple-element.74, ...), kind=kLoop, calls=%fused_computation.4 | loop fusion | flops 72548352 | bytes 155715808 | tf_op jit(solution)/shard_map/vmap()/add | solution.py:42
  126.0 113.4 %while.1 = (s32[]{:T(128)}, f32[27,64,1024]{2,1,0:T(8,128)}, s32[32,3]{0,1:T(4,128)S(1)}, f32[32,27,4,128]{3,2,1,0:T(4,128)}, s32[]{:T(128)}) while((s32[]{:T(128)}, f32[27,64,1024]{2,1,0:T(8,128)}, s32[32,3]{0,1:T(4,128)S(1)}, f32[32,27,4,128]{3,2,1,0:T(4,128)}, s32[]{:T(128)}) %tuple.85), condition=%wide.while_cond, body=%wide.while_body.sunk | while | flops 2 | bytes 112233 | solution.py:65
  126.6 3.0 bitcast_dynamic-update-slice_fusion.2
  130.1 3.0 bitcast_dynamic-update-slice_fusion.2
  140.7 3.0 bitcast_dynamic-update-slice_fusion.2
  144.3 3.0 bitcast_dynamic-update-slice_fusion.2
  151.4 3.0 bitcast_dynamic-update-slice_fusion.2
  154.9 3.0 bitcast_dynamic-update-slice_fusion.2
  165.5 3.0 bitcast_dynamic-update-slice_fusion.2
  169.1 3.0 bitcast_dynamic-update-slice_fusion.2
  176.1 3.0 bitcast_dynamic-update-slice_fusion.2
  179.7 3.0 bitcast_dynamic-update-slice_fusion.2
  183.3 3.0 bitcast_dynamic-update-slice_fusion.2
  186.8 3.0 bitcast_dynamic-update-slice_fusion.2
  190.4 3.0 bitcast_dynamic-update-slice_fusion.2
  193.9 3.0 bitcast_dynamic-update-slice_fusion.2
  197.5 3.0 bitcast_dynamic-update-slice_fusion.2
  201.0 3.0 bitcast_dynamic-update-slice_fusion.2
  204.6 3.0 bitcast_dynamic-update-slice_fusion.2
  208.1 3.0 bitcast_dynamic-update-slice_fusion.2
  211.7 3.0 bitcast_dynamic-update-slice_fusion.2
  218.8 3.0 bitcast_dynamic-update-slice_fusion.2
  222.3 3.0 bitcast_dynamic-update-slice_fusion.2
  229.3 3.0 bitcast_dynamic-update-slice_fusion.2
  232.8 3.0 bitcast_dynamic-update-slice_fusion.2
  243.7 41.0 %custom-call.11 = f32[16,28,28]{2,1,0:T(8,128)S(1)} custom-call(f32[16,28,28]{2,1,0:T(8,128)S(1)} %fusion.35), custom_call_target="Cholesky" | custom-call | tf_op jit(solution)/shard_map/while/body/eval_jaxpr/jit(cholesky)/cholesky | solution.py:93
  285.0 34.7 %custom-call.12 = f32[16,1,28,28]{2,3,1,0:T(8,128)S(1)} custom-call(f32[16,1,28,28]{3,2,1,0:T(8,128)S(1)} %select_bitcast_fusion), custom_call_target="InvertDiagBlocksLowerTriangular" | custom-call | tf_op jit(solution)/shard_map/while/body/eval_jaxpr/triangular_solve | solution.py:103
  324.7 5.9 %all-to-all-start.2 = ((f32[32,4,128]{2,1,0:T(4,128)}), f32[32,4,128]{2,1,0:T(4,128)S(1)}, u32[]{:S(2)}, u32[]{:S(2)}) async-start(f32[32,4,128]{2,1,0:T(4,128)} %reshape.203), calls=%async_computation.2 | async-start | bytes 131072 | tf_op jit(solution)/shard_map/all_to_all | solution.py:168
  330.7 6.9 %all-to-all-done.2 = f32[32,4,128]{2,1,0:T(4,128)S(1)} async-done(((f32[32,4,128]{2,1,0:T(4,128)}), f32[32,4,128]{2,1,0:T(4,128)S(1)}, u32[]{:S(2)}, u32[]{:S(2)}) %all-to-all-start.2) | async-done | bytes 65568 | tf_op jit(solution)/shard_map/all_to_all | solution.py:168
  (130 shorter events, 73.6 us)
Async XLA Ops:
  0.8 29.1 %collective-permute-start = (f32[64,10]{1,0:T(8,128)S(1)}, f32[64,10]{1,0:T(8,128)S(1)}, u32[]{:S(2)}, u32[]{:S(2)}) collective-permute-start(f32[64,10]{1,0:T(8,128)S(1)} %get-tuple-element.66), channel_id=1, source_target_pairs={{0,1},{1,2},{2,3},{3,4},{4,5},{5,6},{6,7},{7,8},{8,9},{9,10},{10,1... | collective-permute-start | bytes 7688 | tf_op jit(solution)/shard_map/ppermute | solution.py:24
  3.2 26.7 %collective-permute-start.1 = (f32[64,10]{1,0:T(8,128)S(1)}, f32[64,10]{1,0:T(8,128)S(1)}, u32[]{:S(2)}, u32[]{:S(2)}) collective-permute-start(f32[64,10]{1,0:T(8,128)S(1)} %get-tuple-element.65), channel_id=1, source_target_pairs={{1,0},{2,1},{3,2},{4,3},{5,4},{6,5},{7,6},{8,7},{9,8},{10,9},{11,1... | collective-permute-start | bytes 7688 | tf_op jit(solution)/shard_map/ppermute | solution.py:26
  7.7 15.8 %all-to-all-start.1 = ((f32[16,2,3]{2,1,0:T(2,128)}), f32[16,2,3]{2,1,0:T(2,128)S(1)}, u32[]{:S(2)}, u32[]{:S(2)}) async-start(f32[16,2,3]{2,1,0:T(2,128)} %bitcast.50), calls=%async_computation.1 | async-start | bytes 32768 | tf_op jit(solution)/shard_map/all_to_all | solution.py:144
  23.5 296.2 %all-to-all-start = ((f32[32,4,128]{2,1,0:T(4,128)}), f32[32,4,128]{2,1,0:T(4,128)S(1)}, u32[]{:S(2)}, u32[]{:S(2)}) async-start(f32[32,4,128]{2,1,0:T(4,128)} %copy.40), calls=%async_computation | async-start | bytes 131072 | tf_op jit(solution)/shard_map/all_to_all | solution.py:143
  239.3 91.3 %copy-start = (s32[16,1]{0,1:T(1,128)S(1)}, s32[16,1]{0,1:T(1,128)}, u32[]{:S(2)}) copy-start(s32[16,1]{0,1:T(1,128)} %param.11) | copy-start | bytes 196
  324.7 12.8 %all-to-all-start.2 = ((f32[32,4,128]{2,1,0:T(4,128)}), f32[32,4,128]{2,1,0:T(4,128)S(1)}, u32[]{:S(2)}, u32[]{:S(2)}) async-start(f32[32,4,128]{2,1,0:T(4,128)} %reshape.203), calls=%async_computation.2 | async-start | bytes 131072 | tf_op jit(solution)/shard_map/all_to_all | solution.py:168
where the time goes:
time: 341 us; the launch traced here: 338 us
  other arithmetic  171 us (50%)
  local copies, waits for them, and re-layouts  126 us (37%)
  starting transfers between devices  24.4 us (7%)
  matrix products  9.49 us (3%)
  waiting for transfers between devices  7.37 us (2%)
    gather x96, local copies, waits for them, and re-layouts  113 us
    add x1, other arithmetic, filter_field(): result + row_taps[shift_tap] * across[shift_tap:shift_tap + out_rows, :]  73.2 us
    another operation x4, other arithmetic, factor_of(): return jnp.linalg.cholesky(pair_normal)  41.2 us
    another operation x3, other arithmetic, finish_fit(): lax.linalg.triangular_solve(factor, inner, left_side=True, lower=True, tr...  34.8 us
    add x1, other arithmetic, filter_field(): across + col_taps[shift_tap] * padded[:, shift_tap:shift_tap + out_cols]  19.8 us
    all_to_all x1, starting transfers between devices, on_device(): lax.all_to_all(slot_info, 'patch', split_axis=0, concat_axis=0, tiled=True)  9.29 us
    all_to_all x1, waiting for transfers between devices, on_device(): lax.all_to_all(residuals, 'patch', split_axis=0, concat_axis=0, tiled=True)  6.87 us
  transfers between devices with their start and end apart: 5, of which 2 were waited for; matrix products, arithmetic and copies ran while one was open for 89% of the time, Pallas kernels for 0%

commit v1 on v0

v1 whole, which is shorter than its diff:
```python
import jax
import jax.numpy as jnp
from jax import lax
from jax.experimental import pallas as pl
from jax.experimental.pallas import tpu as pltpu
from jax.sharding import PartitionSpec as P

CAP = 2
STAMP_HALF = 10
RIDGE = 1.0
LANES = 128
SUBS = 8
VISITS = 16

F32 = jnp.float32
BF16 = jnp.bfloat16
NT = (((1,), (1,)), ((), ()))


def iota(shape, dim):
    return lax.broadcasted_iota(jnp.int32, shape, dim)


def split(x):
    high = x.astype(BF16)
    return high, (x - high.astype(F32)).astype(BF16)


INFO_ROW = 2


def pack_kernel(own_ref, dest_ref, row_ref, col_ref, first_ref, last_ref, science_ref, out_ref, count, source):
    peers = out_ref.shape[0]
    strips = science_ref.shape[0]
    own = own_ref[0]

    def clear(d, _):
        count[d] = 0
        for r in range(CAP):
            source[CAP * d + r] = -1
        return 0

    lax.fori_loop(0, peers, clear, 0, unroll=min(peers, 16))

    def place(s, _):
        d = dest_ref[s, 0]
        rank = count[d]
        source[CAP * d + rank] = s
        count[d] = rank + 1
        return 0

    lax.fori_loop(0, strips, place, 0, unroll=min(strips, 16))

    edges = jnp.concatenate([first_ref[...], last_ref[...]], axis=0).T
    lane = iota((SUBS, LANES), 1)
    sub = iota((SUBS, LANES), 0)
    rows = LANES // 2
    low = lane < rows
    head = jnp.where(low, edges[0:8], pltpu.roll(edges[8:16], rows, 1))
    tail = jnp.where(low, pltpu.roll(edges[120:128], rows, 1), edges[112:120])
    info_here = (~low) & (sub == INFO_ROW)

    def fill(d, _):
        halo = jnp.where(d == own + 1, tail, head)
        info = jnp.zeros((SUBS, LANES), F32)
        parts = []
        for r in range(CAP):
            s = source[CAP * d + r]
            live = s >= 0
            at = jnp.maximum(s, 0)
            strip = science_ref[at]
            parts.append(jnp.where(live, strip, 0.0))
            values = (row_ref[at], col_ref[at], jnp.int32(1))
            for j, value in enumerate(values):
                value = jnp.where(live, value, 0).astype(F32)
                info = jnp.where(lane == rows + 3 * r + j, value, info)
        out_ref[d, 0:SUBS, :] = jnp.concatenate(parts, axis=0)
        out_ref[d, SUBS : 2 * SUBS, :] = jnp.where(info_here, info, halo)
        return 0

    lax.fori_loop(0, peers, fill, 0, unroll=min(peers, 16))


def prep_kernel(own_ref, rows_ref, cols_ref, stamp_r_ref, stamp_c_ref, col_taps_ref, row_taps_ref, mask_ref, pad_c, pad_r):
    bases, taps = rows_ref.shape
    own = own_ref[0]
    blocks, sub_rows, _ = mask_ref.shape
    sub_rows = sub_rows - SUBS
    sub_cols = blocks * LANES
    centre_r = stamp_r_ref[pl.ds(own, 1), :]
    centre_c = stamp_c_ref[pl.ds(own, 1), :]
    stamps = centre_r.shape[1]
    row_hit = (jnp.abs(iota((sub_rows, stamps), 0) - centre_r) <= STAMP_HALF).astype(F32).astype(BF16)
    col_hit = (jnp.abs(iota((sub_cols, stamps), 0) - centre_c) <= STAMP_HALF).astype(F32).astype(BF16)
    counts = lax.dot_general(row_hit, col_hit, NT, preferred_element_type=F32)
    for c in range(blocks):
        mask_ref[c, 0:sub_rows, :] = jnp.minimum(counts[:, LANES * c : LANES * (c + 1)], 1.0)
        mask_ref[c, sub_rows:, :] = jnp.zeros((SUBS, LANES), F32)
    pad_c[...] = jnp.zeros_like(pad_c)
    pad_r[...] = jnp.zeros_like(pad_r)
    pad_c[0:bases, 0:taps] = cols_ref[...]
    pad_r[0:bases, 0:taps] = rows_ref[...]
    full = pad_r[...]
    high = full.astype(BF16).astype(F32)
    base = high + pltpu.roll(high, 32, 1) + pltpu.roll(full - high, 64, 1)
    wide = jnp.concatenate([base, jnp.zeros_like(base)], axis=1)
    lower = iota((SUBS, 2 * LANES), 0) < SUBS // CAP
    for k in range(bases):
        row = jnp.broadcast_to(wide[k : k + 1, :], (SUBS, 2 * LANES))
        row = pltpu.roll(row, 0, 1, stride=1, stride_axis=0)
        row = jnp.where(lower, row, pltpu.roll(row, 96 - SUBS // CAP, 1))
        row_taps_ref[SUBS * k : SUBS * (k + 1), :] = row
    row_at = iota((LANES, LANES), 0)
    lane_at = iota((LANES, LANES), 1)
    inside = lane_at >= row_at

    def column(k, _):
        ring = jnp.broadcast_to(pad_c[pl.ds(k, 1), :], (LANES, LANES))
        ring = pltpu.roll(ring, 0, 1, stride=1, stride_axis=0)
        for half, kept in ((0, inside), (1, ~inside)):
            piece_h, piece_l = split(jnp.where(kept, ring, 0.0))
            col_taps_ref[k, 0:LANES, LANES * half : LANES * (half + 1)] = piece_h
            col_taps_ref[k, LANES : 2 * LANES, LANES * half : LANES * (half + 1)] = piece_l
        return 0

    lax.fori_loop(0, bases, column, 0, unroll=3)


def main_kernel(
    own_ref, arrived_ref, left_ref, right_ref, template_ref, col_taps_hbm, row_taps_ref, mask_ref, out_ref,
    frame, info_v, info_s, taps_v, weight, field, design, weighted, gram, copy_sem, taps_sem,
):
    step = pl.program_id(0)
    own = own_ref[0]
    peers = own_ref[1]
    bases = col_taps_hbm.shape[0]
    columns = bases + 1
    rows = template_ref.shape[0]
    blocks = template_ref.shape[1] // LANES
    per = VISITS * SUBS

    info_v[...] = arrived_ref[:, SUBS + INFO_ROW, :]
    info_copy = pltpu.make_async_copy(info_v, info_s, copy_sem)
    info_copy.start()

    @pl.when(step == 0)
    def _():
        taps_copy = pltpu.make_async_copy(col_taps_hbm, taps_v, taps_sem)
        taps_copy.start()
        lane = iota((SUBS, LANES), 1)
        left = jnp.where(own > 0, left_ref[0], 0.0)
        right = jnp.where(own < peers - 1, right_ref[0], 0.0)
        gap = jnp.zeros((LANES - 4 * SUBS, LANES), F32)
        halo = jnp.concatenate([pltpu.roll(right, 64, 1), right, gap, pltpu.roll(left, 64, 1), left], axis=0).T
        frame[:, 0:16, :] = jnp.zeros((blocks + 1, 16, LANES), F32)
        frame[:, 16 + rows :, :] = jnp.zeros((blocks + 1, frame.shape[1] - 16 - rows, LANES), F32)
        shift = 10
        for t in range(rows // SUBS):
            at = slice(SUBS * t, SUBS * (t + 1))
            before = pltpu.roll(halo[at], shift, 1)
            for c in range(blocks + 1):
                if c < blocks:
                    here = template_ref[at, LANES * c : LANES * (c + 1)]
                else:
                    here = halo[rows + SUBS * t : rows + SUBS * (t + 1)]
                here = pltpu.roll(here, shift, 1)
                frame[c, 16 + SUBS * t : 16 + SUBS * (t + 1), :] = jnp.where(lane < shift, before, here)
                before = here
        design[bases, :, :] = jnp.ones((per, LANES), F32)
        weighted[columns + 1 :, :, :] = jnp.zeros((32 - columns - 1, per, LANES), F32)
        taps_copy.wait()

    info_copy.wait()
    row_taps = row_taps_ref[...].astype(BF16)[:, 0:192]

    def convolve_rows(pair, _):
        outs = []
        for half in range(2):
            b = 2 * pair + half
            terms = []
            masks = []
            for r in range(CAP):
                first = info_s[b, 64 + 3 * r].astype(jnp.int32)
                block = info_s[b, 65 + 3 * r].astype(jnp.int32)
                live = info_s[b, 66 + 3 * r]
                sides = [frame[block + side, pl.ds(first + 6, 32), :] for side in range(2)]
                window = jnp.concatenate(sides, axis=1)
                high, low = split(window)
                terms += [high, low, high]
                masks.append(mask_ref[block, pl.ds(first, SUBS), :][0 : SUBS // CAP] * live)
            weight[pl.ds(pl.multiple_of(SUBS * b, SUBS), SUBS), :] = jnp.concatenate(masks, axis=0)
            tall = jnp.concatenate(terms, axis=0)
            across = lax.dot_general(row_taps, tall, (((1,), (0,)), ((), ())), preferred_element_type=F32)
            outs.append(across.reshape(bases, SUBS, 2 * LANES))
        both = jnp.concatenate(outs, axis=1)
        high, low = split(both)
        at = pl.multiple_of(2 * SUBS * pair, 2 * SUBS)
        field[:, pl.ds(at, 2 * SUBS), :] = high
        field[:, pl.ds(per + at, 2 * SUBS), :] = low
        return 0

    lax.fori_loop(0, VISITS // 2, convolve_rows, 0)

    hits = weight[...]

    def convolve_cols(k, _):
        out = lax.dot_general(field[k], taps_v[k], NT, preferred_element_type=F32)
        conv = (out[0:per, LANES:] + out[per:, 0:LANES]) + out[0:per, 0:LANES]
        design[k] = conv
        weighted[k] = conv * hits
        return 0

    lax.fori_loop(0, bases, convolve_cols, 0, unroll=3)
    science = arrived_ref[:, 0:SUBS, :].reshape(per, LANES)
    weighted[bases] = hits
    weighted[columns] = science * hits

    def gram_of(b, _):
        rows_of = []
        for q in range(SUBS):
            rows_of.append(weighted[:, SUBS * b + q, :])
        flat = jnp.concatenate(rows_of, axis=1)
        high, low = split(flat)
        both = jnp.concatenate([high, low], axis=0)
        out = lax.dot_general(both, both, NT, preferred_element_type=F32)
        cross = out[0:32, 32:64] + out[32:64, 0:32]
        gram[b, :, 0:32] = cross + out[0:32, 0:32]
        return 0

    lax.fori_loop(0, VISITS, gram_of, 0)

    lane = iota((LANES, LANES), 1)
    groups = []
    for g in range(4):
        picked = [gram[:, 8 * g + jj, :] for jj in range(8)]
        stacked = jnp.concatenate(picked, axis=0)
        groups.append(stacked.T[0:32])
    lane = iota((32, LANES), 1)
    sub = iota((32, LANES), 0)
    for g in range(4):
        diagonal = (sub == 8 * g + lane // VISITS) & (sub < columns)
        groups[g] = groups[g] + jnp.where(diagonal, RIDGE, 0.0)
    visit = lane % VISITS
    for k in range(columns):
        factor = jnp.take_along_axis(groups[k // 8], visit + VISITS * (k % 8), axis=1)
        pivot = factor[k : k + 1, :]
        inverse = 1.0 / pivot
        scaled = jnp.where(sub == k, (pivot - 1.0) * inverse, factor * inverse)
        for g in range(k // 8, 4):
            groups[g] = groups[g] - scaled * groups[g][k : k + 1, :]
    target = columns
    answer = jnp.take_along_axis(groups[target // 8], lane // SUBS + VISITS * (target % 8), axis=1)
    coeff = jnp.concatenate([answer, jnp.zeros((LANES - 32, LANES), F32)], axis=0).T

    residual = science - coeff[:, bases : bases + 1]
    for k in range(bases):
        residual = residual - coeff[:, k : k + 1] * design[k]
    out_ref[...] = residual.reshape(VISITS, SUBS, LANES)


def unpack_kernel(dest_ref, back_ref, out_ref, count):
    peers = back_ref.shape[0]
    strips = out_ref.shape[0]

    def clear(d, _):
        count[d] = 0
        return 0

    lax.fori_loop(0, peers, clear, 0, unroll=min(peers, 16))

    def pick(s, _):
        d = dest_ref[s, 0]
        rank = count[d]
        count[d] = rank + 1
        both = back_ref[d]
        half = SUBS // CAP
        out_ref[s] = jnp.where(rank == 0, both[0:half], both[half:SUBS])
        return 0

    lax.fori_loop(0, strips, pick, 0, unroll=min(strips, 16))


VMEM = pl.BlockSpec(memory_space=pltpu.VMEM)
SMEM = pl.BlockSpec(memory_space=pltpu.SMEM)
ANY = pl.BlockSpec(memory_space=pl.ANY)


def on_device(
    template, science, dest, row_offset, col_block, basis_rows, basis_cols, stamp_rows, stamp_cols
):
    peers = lax.axis_size("patch")
    own = lax.axis_index("patch").astype(jnp.int32)
    rows, cols = template.shape
    strips, strip_rows, block_cols = science.shape
    bases = basis_rows.shape[0]
    place = jnp.stack([own, jnp.int32(peers)])
    last = cols // LANES - 1

    payload = pl.pallas_call(
        pack_kernel,
        grid=(1,),
        out_shape=jax.ShapeDtypeStruct((peers, 2 * SUBS, LANES), F32),
        in_specs=[
            SMEM, SMEM, SMEM, SMEM,
            pl.BlockSpec((rows, LANES), lambda i: (0, 0)),
            pl.BlockSpec((rows, LANES), lambda i: (0, last)),
            VMEM,
        ],
        out_specs=VMEM,
        scratch_shapes=[pltpu.SMEM((peers,), jnp.int32), pltpu.SMEM((CAP * peers,), jnp.int32)],
        name="pack",
    )(place, dest, row_offset, col_block, template, template, science)

    arrived = lax.all_to_all(payload, "patch", split_axis=0, concat_axis=0, tiled=True)

    col_taps, row_taps, mask = pl.pallas_call(
        prep_kernel,
        out_shape=(
            jax.ShapeDtypeStruct((bases, 2 * LANES, 2 * LANES), BF16),
            jax.ShapeDtypeStruct((bases * SUBS, 2 * LANES), F32),
            jax.ShapeDtypeStruct((cols // LANES, rows + SUBS, LANES), F32),
        ),
        in_specs=[SMEM, VMEM, VMEM, VMEM, VMEM],
        out_specs=(VMEM, VMEM, VMEM),
        scratch_shapes=[pltpu.VMEM((32, LANES), F32), pltpu.VMEM((32, LANES), F32)],
        name="prep",
    )(place, basis_rows, basis_cols, stamp_rows, stamp_cols)

    per = VISITS * SUBS
    residual = pl.pallas_call(
        main_kernel,
        grid_spec=pltpu.PrefetchScalarGridSpec(
            num_scalar_prefetch=1,
            grid=(peers // VISITS,),
            in_specs=[
                pl.BlockSpec((VISITS, 2 * SUBS, LANES), lambda i, at: (i, 0, 0)),
                pl.BlockSpec((1, SUBS, LANES), lambda i, at: (jnp.maximum(at[0] - 1, 0), 1, 0)),
                pl.BlockSpec((1, SUBS, LANES), lambda i, at: (jnp.minimum(at[0] + 1, at[1] - 1), 1, 0)),
                pl.BlockSpec((rows, cols), lambda i, at: (0, 0)),
                ANY,
                pl.BlockSpec((bases * SUBS, 2 * LANES), lambda i, at: (0, 0)),
                pl.BlockSpec((cols // LANES, rows + SUBS, LANES), lambda i, at: (0, 0, 0)),
            ],
            out_specs=pl.BlockSpec((VISITS, SUBS, LANES), lambda i, at: (i, 0, 0)),
            scratch_shapes=[
                pltpu.VMEM((cols // LANES + 1, rows + 40, LANES), F32),
                pltpu.VMEM((VISITS, LANES), F32),
                pltpu.SMEM((VISITS, LANES), F32),
                pltpu.VMEM((bases, 2 * LANES, 2 * LANES), BF16),
                pltpu.VMEM((per, LANES), F32),
                pltpu.VMEM((bases, 2 * per, 2 * LANES), BF16),
                pltpu.VMEM((bases + 1, per, LANES), F32),
                pltpu.VMEM((32, per, LANES), F32),
                pltpu.VMEM((VISITS, 32, LANES), F32),
                pltpu.SemaphoreType.DMA,
                pltpu.SemaphoreType.DMA,
            ],
        ),
        out_shape=jax.ShapeDtypeStruct((peers, SUBS, LANES), F32),
        name="fit",
    )(place, arrived, arrived, arrived, template, col_taps, row_taps, mask)

    returned = lax.all_to_all(residual, "patch", split_axis=0, concat_axis=0, tiled=True)

    return pl.pallas_call(
        unpack_kernel,
        out_shape=jax.ShapeDtypeStruct(science.shape, F32),
        in_specs=[SMEM, VMEM],
        out_specs=VMEM,
        scratch_shapes=[pltpu.SMEM((peers,), jnp.int32)],
        name="unpack",
    )(dest, returned)


def solution(mesh):
    placed = (
        P(None, ("groups", "patch")),
        P(("groups", "patch"), None, None),
        P(("groups", "patch"), None),
        P(("groups", "patch")),
        P(("groups", "patch")),
        P(),
        P(),
        P("groups", None),
        P("groups", None),
    )
    return jax.shard_map(
        on_device,
        mesh=mesh,
        in_specs=placed,
        out_specs=P(("groups", "patch"), None, None),
        check_vma=False,
    )
```

time: 341 us -> 52.5 us (0.15)
  other arithmetic: 171 us -> 0.59 us
  local copies, waits for them, and re-layouts: 126 us -> 4.76 us
  Pallas kernels: 0 us -> 26.1 us
  starting transfers between devices: 24.4 us -> 7.41 us
  blocking collectives: 0 us -> 12.1 us
  matrix products: 9.49 us -> 0 us
  waiting for transfers between devices: 7.37 us -> 0.9 us
    gather x96 -> x0, local copies, waits for them, and re-layouts: 113 us -> none
    add x6 -> x0, other arithmetic: 93.8 us -> none  [the longest x1 73.2 us: filter_field(): result + row_taps[shift_tap] * across[shift_tap:shift_tap + out_rows, :]]
    another operation x7 -> x1, other arithmetic: 76 us -> 0.59 us  [on_device(): place = jnp.stack([own, jnp.int32(peers)])]
    pallas_call x0 -> x4, Pallas kernels: none -> 26.1 us  [the longest x1 18.5 us: on_device(): pl.pallas_call(main_kernel, grid_spec=pltpu.PrefetchScalarGridSpec(num_sc...]
    all_to_all x3 -> x1, starting transfers between devices: 20.7 us -> 7.41 us  [on_device(): lax.all_to_all(payload, 'patch', split_axis=0, concat_axis=0, tiled=True)]
    all_to_all x0 -> x1, blocking collectives: none -> 12.1 us  [on_device(): lax.all_to_all(residual, 'patch', split_axis=0, concat_axis=0, tiled=True)]
    dot_general x6 -> x0, matrix products: 7.08 us -> none  [the longest x1 2.11 us: factor_of(): normal = jnp.einsum('skp,slp->skl', weighted, design, precision=HIGH)]
    all_to_all x3 -> x1, waiting for transfers between devices: 7.36 us -> 0.9 us  [on_device(): lax.all_to_all(payload, 'patch', split_axis=0, concat_axis=0, tiled=True)]
  transfers between devices with their start and end apart: 5 -> 1, of which waited for: 2 -> 1; matrix products, arithmetic and copies ran while one was open for 89% -> 5% of each run, Pallas kernels for 0% -> 8%
where the time goes in v1:
time: 52.5 us; the launch traced here: 51.9 us
  Pallas kernels  26.1 us (50%)
  blocking collectives  12.1 us (23%)
  starting transfers between devices  7.41 us (14%)
  local copies, waits for them, and re-layouts  4.76 us (9%)
  waiting for transfers between devices  0.9 us (2%)
  other arithmetic  0.59 us (1%)
    pallas_call x1, Pallas kernels, on_device(): pl.pallas_call(main_kernel, grid_spec=pltpu.PrefetchScalarGridSpec(num_sc...  18.5 us
    all_to_all x1, blocking collectives, on_device(): lax.all_to_all(residual, 'patch', split_axis=0, concat_axis=0, tiled=True)  12.1 us
    all_to_all x1, starting transfers between devices, on_device(): lax.all_to_all(payload, 'patch', split_axis=0, concat_axis=0, tiled=True)  7.41 us
    unnamed x5, local copies, waits for them, and re-layouts  4.76 us
    pallas_call x1, Pallas kernels, on_device(): pl.pallas_call(prep_kernel, out_shape=(jax.ShapeDtypeStruct((bases, 2 * L...  4.21 us
    pallas_call x1, Pallas kernels, on_device(): pl.pallas_call(pack_kernel, grid=(1,), out_shape=jax.ShapeDtypeStruct((pe...  1.86 us
    pallas_call x1, Pallas kernels, on_device(): pl.pallas_call(unpack_kernel, out_shape=jax.ShapeDtypeStruct(science.shap...  1.55 us
  transfers between devices with their start and end apart: 1, of which 1 were waited for; matrix products, arithmetic and copies ran while one was open for 5% of the time, Pallas kernels for 8%

profile of v1, /device:TPU:0, one launch (start us, length us, event | category | flops | bytes accessed | tf_op | source)
XLA Modules:
  0.0 51.9 jit_solution(3816548603140937965)
XLA Ops:
  0.0 1.3 %copy.13.dest_ref = s32[16,1]{1,0:T(8,128)} copy(s32[16,1]{0,1:T(1,128)} %param.11) | data formatting | bytes 128 | tf_op args[2]
  1.3 0.6 %pad_add_fusion.own_ref = s32[2]{0:T(128)} fusion(s32[1]{0:T(128)} %constant.1.clone.1, s32[1]{0:T(128)} %bitcast), kind=kLoop, calls=%fused_computation | loop fusion | flops 2 | bytes 16 | tf_op jit(solution)/shard_map/stack | solution.py:296
  1.9 1.9 %pack.1 = f32[16,16,128]{2,1,0:T(8,128)} custom-call(s32[2]{0:T(128)} %pad_add_fusion.own_ref, s32[16,1]{1,0:T(8,128)} %copy.13.dest_ref, s32[16]{0:T(128)} %row_ref.1, s32[16]{0:T(128)} %col_ref.1, f32[64,1024]{1,0:T(8,128)} %template_ref.1, f32[64,1024]{1,0:T(8,128)} %template_ref.1, f32[16,4,128]{2,1,0:T(4,128)} %science_ref.1), custom_call_target="tpu_custom_call" | custom-call | tf_op jit(solution)/shard_map/pack/pallas_call | solution.py:299
  3.8 7.4 %all-to-all-start = ((f32[16,16,128]{2,1,0:T(8,128)}), f32[16,16,128]{2,1,0:T(8,128)S(1)}, u32[]{:S(2)}, u32[]{:S(2)}) async-start(f32[16,16,128]{2,1,0:T(8,128)} %pack.1), calls=%async_computation | async-start | bytes 262144 | tf_op jit(solution)/shard_map/all_to_all | solution.py:314
  11.2 1.4 %copy.11.rows_ref = f32[27,21]{1,0:T(8,128)} copy(f32[27,21]{0,1:T(8,128)} %param.14) | data formatting | bytes 4536 | tf_op args[5]
  12.6 1.4 %copy.12.cols_ref = f32[27,21]{1,0:T(8,128)} copy(f32[27,21]{0,1:T(8,128)} %param.15) | data formatting | bytes 4536 | tf_op args[6]
  14.0 4.2 %prep.1 = (bf16[27,256,256]{2,1,0:T(8,128)(2,1)}, f32[216,256]{1,0:T(8,128)}, f32[8,72,128]{2,1,0:T(8,128)}) custom-call(s32[2]{0:T(128)} %pad_add_fusion.own_ref, f32[27,21]{1,0:T(8,128)} %copy.11.rows_ref, f32[27,21]{1,0:T(8,128)} %copy.12.cols_ref, s32[16,24]{1,0:T(8,128)} %stamp_r_ref.1, s32[16,24]{1,0:T(8,128)} %stamp_c_ref.1), custom_call_target="tpu_custom_call" | custom-call | tf_op jit(solution)/shard_map/prep/pallas_call | solution.py:316
  18.2 0.9 %all-to-all-done.arrived_ref.left_ref.right_ref = f32[16,16,128]{2,1,0:T(8,128)S(1)} async-done(((f32[16,16,128]{2,1,0:T(8,128)}), f32[16,16,128]{2,1,0:T(8,128)S(1)}, u32[]{:S(2)}, u32[]{:S(2)}) %all-to-all-start) | async-done | bytes 131104 | tf_op jit(solution)/shard_map/all_to_all | solution.py:314
  19.1 0.0 copy-start
  19.1 0.7 %copy-done = f32[16,16,128]{2,1,0:T(8,128)} copy-done((f32[16,16,128]{2,1,0:T(8,128)}, f32[16,16,128]{2,1,0:T(8,128)S(1)}, u32[]{:S(2)}) %copy-start) | copy-done | bytes 131096
  19.8 18.5 %fit.1 = f32[16,8,128]{2,1,0:T(8,128)} custom-call(s32[2]{0:T(128)} %pad_add_fusion.own_ref, f32[16,16,128]{2,1,0:T(8,128)} %copy-done, f32[16,16,128]{2,1,0:T(8,128)} %copy-done, f32[16,16,128]{2,1,0:T(8,128)} %copy-done, f32[64,1024]{1,0:T(8,128)} %template_ref.1, bf16[27,256,256]{2,1,0:T(8,128)(2,1)} %get-tuple-element.8.col_taps_hbm, ...), custom_call_target="tpu_custom_call" | custom-call | tf_op jit(solution)/shard_map/fit/pallas_call | solution.py:330
  38.2 12.1 %all_to_all.10.back_ref = f32[16,8,128]{2,1,0:T(8,128)} all-to-all(f32[16,8,128]{2,1,0:T(8,128)} %fit.1), channel_id=1, replica_groups=mesh['groups'=2,'patch'=16] {'patch'}, dimensions={0} | all-to-all | bytes 131072 | tf_op jit(solution)/shard_map/all_to_all | solution.py:363
  50.3 1.5 %unpack.1 = f32[16,4,128]{2,1,0:T(4,128)} custom-call(s32[16,1]{1,0:T(8,128)} %copy.13.dest_ref, f32[16,8,128]{2,1,0:T(8,128)} %all_to_all.10.back_ref), custom_call_target="tpu_custom_call" | custom-call | tf_op jit(solution)/shard_map/unpack/pallas_call | solution.py:365
Async XLA Ops:
  3.8 15.3 %all-to-all-start = ((f32[16,16,128]{2,1,0:T(8,128)}), f32[16,16,128]{2,1,0:T(8,128)S(1)}, u32[]{:S(2)}, u32[]{:S(2)}) async-start(f32[16,16,128]{2,1,0:T(8,128)} %pack.1), calls=%async_computation | async-start | bytes 262144 | tf_op jit(solution)/shard_map/all_to_all | solution.py:314
  19.1 0.7 %copy-start = (f32[16,16,128]{2,1,0:T(8,128)}, f32[16,16,128]{2,1,0:T(8,128)S(1)}, u32[]{:S(2)}) copy-start(f32[16,16,128]{2,1,0:T(8,128)S(1)} %all-to-all-done.arrived_ref.left_ref.right_ref) | copy-start | bytes 393220

commit v2 on v1

v2 whole, which is shorter than its diff:
```python
import jax
import jax.numpy as jnp
from jax import lax
from jax.experimental import pallas as pl
from jax.experimental.pallas import tpu as pltpu
from jax.sharding import PartitionSpec as P

CAP = 2
STAMP_HALF = 10
RIDGE = 1.0
LANES = 128
SUBS = 8
VISITS = 16
PITCH = VISITS * SUBS + 8

F32 = jnp.float32
BF16 = jnp.bfloat16
NT = (((1,), (1,)), ((), ()))


def iota(shape, dim):
    return lax.broadcasted_iota(jnp.int32, shape, dim)


def split(x):
    high = x.astype(BF16)
    return high, (x - high.astype(F32)).astype(BF16)


INFO_ROW = 2
SHIFT = 10
TOP = 16


def pack_kernel(dest_ref, row_ref, col_ref, first_ref, last_ref, science_ref, out_ref, count, source):
    peers = out_ref.shape[0]
    strips = science_ref.shape[0]
    own = lax.axis_index("patch")

    def clear(d, _):
        count[d] = 0
        for r in range(CAP):
            source[CAP * d + r] = -1
        return 0

    lax.fori_loop(0, peers, clear, 0, unroll=min(peers, 16))

    def place(s, _):
        d = dest_ref[s]
        rank = count[d]
        source[CAP * d + rank] = s
        count[d] = rank + 1
        return 0

    lax.fori_loop(0, strips, place, 0, unroll=min(strips, 16))

    edges = jnp.concatenate([first_ref[...], last_ref[...]], axis=0).T
    lane = iota((SUBS, LANES), 1)
    sub = iota((SUBS, LANES), 0)
    rows = LANES // 2
    low = lane < rows
    head = jnp.where(low, edges[0:8], pltpu.roll(edges[8:16], rows, 1))
    tail = jnp.where(low, pltpu.roll(edges[120:128], rows, 1), edges[112:120])
    info_here = (~low) & (sub == INFO_ROW)

    def fill(d, _):
        halo = jnp.where(d == own + 1, tail, head)
        info = jnp.zeros((SUBS, LANES), F32)
        parts = []
        for r in range(CAP):
            s = source[CAP * d + r]
            live = s >= 0
            at = jnp.maximum(s, 0)
            strip = science_ref[at]
            parts.append(jnp.where(live, strip, 0.0))
            values = (row_ref[at], col_ref[at], jnp.int32(1))
            for j, value in enumerate(values):
                value = jnp.where(live, value, 0).astype(F32)
                info = jnp.where(lane == rows + 3 * r + j, value, info)
        out_ref[d, 0:SUBS, :] = jnp.concatenate(parts, axis=0)
        out_ref[d, SUBS : 2 * SUBS, :] = jnp.where(info_here, info, halo)
        return 0

    lax.fori_loop(0, peers, fill, 0, unroll=min(peers, 16))


def prep_kernel(
    template_ref, rows_ref, cols_ref, stamp_r_ref, stamp_c_ref, frame_ref, col_taps_ref, row_taps_ref, mask_ref, pad_c, pad_t
):
    taps, bases = rows_ref.shape
    own = lax.axis_index("patch")
    rows = template_ref.shape[0]
    blocks = frame_ref.shape[0]
    frame_ref[:, 0:TOP, :] = jnp.zeros((blocks, TOP, LANES), F32)
    frame_ref[:, TOP + rows :, :] = jnp.zeros((blocks, frame_ref.shape[1] - TOP - rows, LANES), F32)
    starts = iota((rows, LANES), 1) < SHIFT
    before = jnp.zeros((rows, LANES), F32)
    for c in range(blocks):
        here = jnp.zeros((rows, LANES), F32)
        if c < blocks - 1:
            here = pltpu.roll(template_ref[:, LANES * c : LANES * (c + 1)], SHIFT, 1)
        frame_ref[c, TOP : TOP + rows, :] = jnp.where(starts, before, here)
        before = here
    blocks, sub_rows, _ = mask_ref.shape
    sub_rows = sub_rows - SUBS
    sub_cols = blocks * LANES
    centre_r = stamp_r_ref[pl.ds(own, 1), :]
    centre_c = stamp_c_ref[pl.ds(own, 1), :]
    stamps = centre_r.shape[1]
    row_hit = (jnp.abs(iota((sub_rows, stamps), 0) - centre_r) <= STAMP_HALF).astype(F32).astype(BF16)
    col_hit = (jnp.abs(iota((sub_cols, stamps), 0) - centre_c) <= STAMP_HALF).astype(F32).astype(BF16)
    counts = lax.dot_general(row_hit, col_hit, NT, preferred_element_type=F32)
    for c in range(blocks):
        mask_ref[c, 0:sub_rows, :] = jnp.minimum(counts[:, LANES * c : LANES * (c + 1)], 1.0)
        mask_ref[c, sub_rows:, :] = jnp.zeros((SUBS, LANES), F32)
    pad_t[...] = jnp.zeros_like(pad_t)
    pad_t[0:taps, 0:bases] = cols_ref[...]
    pad_t[32 : 32 + taps, 0:bases] = rows_ref[...]
    filters = pad_t[...].T
    pad_c[...] = jnp.where(iota((32, LANES), 1) < 32, filters[0:32], 0.0)
    full = jnp.where(iota((32, LANES), 1) < 32, pltpu.roll(filters[0:32], LANES - 32, 1), 0.0)
    high = full.astype(BF16).astype(F32)
    base = high + pltpu.roll(high, 32, 1) + pltpu.roll(full - high, 64, 1)
    wide = jnp.concatenate([base, jnp.zeros_like(base)], axis=1)
    lower = iota((SUBS, 2 * LANES), 0) < SUBS // CAP
    tiles = []
    for k in range(bases):
        row = jnp.broadcast_to(wide[k : k + 1, :], (SUBS, 2 * LANES))
        row = pltpu.roll(row, 0, 1, stride=1, stride_axis=0)
        row = jnp.where(lower, row, pltpu.roll(row, 96 - SUBS // CAP, 1))
        tiles.append(row)
    row_taps_ref[...] = jnp.concatenate(tiles, axis=0).astype(BF16)
    def column(k, _):
        ring = jnp.broadcast_to(pad_c[pl.ds(k, 1), :], (LANES, LANES))
        high, low = split(pltpu.roll(ring, 0, 1, stride=1, stride_axis=0))
        col_taps_ref[k, 0:LANES, :] = high
        col_taps_ref[k, LANES : 2 * LANES, :] = low
        return 0

    lax.fori_loop(0, bases, column, 0, unroll=9)


def main_kernel(
    arrived_ref, frame_ref, col_taps_ref, row_taps_ref, mask_ref, out_ref,
    frame, info_v, info_s, weight, field, design, weighted, gram, info_sem,
):
    own = lax.axis_index("patch")
    peers = arrived_ref.shape[0]
    bases = col_taps_ref.shape[0]
    rows = LANES // 2
    last = frame.shape[0] - 1
    per = VISITS * SUBS

    info_v[...] = arrived_ref[:, SUBS + INFO_ROW, :]
    info_copy = pltpu.make_async_copy(info_v, info_s, info_sem)
    info_copy.start()

    left = jnp.where(own > 0, arrived_ref[jnp.maximum(own - 1, 0), SUBS : 2 * SUBS, :], 0.0)
    right = jnp.where(own < peers - 1, arrived_ref[jnp.minimum(own + 1, peers - 1), SUBS : 2 * SUBS, :], 0.0)
    gap = jnp.zeros((LANES - 4 * SUBS, LANES), F32)
    halo = jnp.concatenate([pltpu.roll(right, 64, 1), right, gap, pltpu.roll(left, 64, 1), left], axis=0).T
    halo = pltpu.roll(halo, SHIFT, 1)
    starts = iota((rows, LANES), 1) < SHIFT
    frame[...] = frame_ref[...]
    frame[0, TOP : TOP + rows, :] = jnp.where(starts, halo[0:rows], frame_ref[0, TOP : TOP + rows, :])
    frame[last, TOP : TOP + rows, :] = jnp.where(starts, frame_ref[last, TOP : TOP + rows, :], halo[rows : 2 * rows])
    columns = bases + 1
    design[bases, :, :] = jnp.ones((per, LANES), F32)
    weighted[PITCH * (columns + 1) :, :] = jnp.zeros((weighted.shape[0] - PITCH * (columns + 1), LANES), F32)
    info_copy.wait()

    def fit_group(group, _):
        fit_visits(
            group, arrived_ref, col_taps_ref, row_taps_ref, mask_ref, out_ref,
            frame, info_s, weight, field, design, weighted, gram,
        )
        return 0

    if peers == VISITS:
        fit_group(0, 0)
    else:
        lax.fori_loop(0, peers // VISITS, fit_group, 0)


def fit_visits(
    group, arrived_ref, col_taps_ref, row_taps_ref, mask_ref, out_ref,
    frame, info_s, weight, field, design, weighted, gram,
):
    bases = col_taps_ref.shape[0]
    columns = bases + 1
    per = VISITS * SUBS
    row_taps = row_taps_ref[:, 0:192]

    def convolve_rows(pair, _):
        outs = []
        for half in range(2):
            b = 2 * pair + half
            visit = group * VISITS + b
            terms = []
            masks = []
            for r in range(CAP):
                first = info_s[visit, 64 + 3 * r].astype(jnp.int32)
                block = info_s[visit, 65 + 3 * r].astype(jnp.int32)
                live = info_s[visit, 66 + 3 * r]
                sides = [frame[block + side, pl.ds(first + 6, 32), :] for side in range(2)]
                window = jnp.concatenate(sides, axis=1)
                high, low = split(window)
                terms += [high, low, high]
                masks.append(mask_ref[block, pl.ds(first, SUBS), :][0 : SUBS // CAP] * live)
            weight[pl.ds(pl.multiple_of(SUBS * b, SUBS), SUBS), :] = jnp.concatenate(masks, axis=0)
            tall = jnp.concatenate(terms, axis=0)
            across = lax.dot_general(row_taps, tall, (((1,), (0,)), ((), ())), preferred_element_type=F32)
            outs.append(across.reshape(bases, SUBS, 2 * LANES))
        both = jnp.concatenate(outs, axis=1)
        high, low = split(both)
        at = pl.multiple_of(2 * SUBS * pair, 2 * SUBS)
        field[:, pl.ds(at, 2 * SUBS), :] = high
        field[:, pl.ds(per + at, 2 * SUBS), :] = low
        return 0

    lax.fori_loop(0, VISITS // 2, convolve_rows, 0, unroll=2)

    hits = weight[...]

    inside = iota((2 * LANES, LANES), 1) >= iota((2 * LANES, LANES), 0) % LANES

    def convolve_cols(k, _):
        ring = col_taps_ref[k]
        none = jnp.zeros_like(ring)
        band = jnp.concatenate([jnp.where(inside, ring, none), jnp.where(inside, none, ring)], axis=1)
        out = lax.dot_general(field[k], band, NT, preferred_element_type=F32)
        conv = (out[0:per, LANES:] + out[per:, 0:LANES]) + out[0:per, 0:LANES]
        design[k] = conv
        weighted[pl.ds(PITCH * k, per), :] = conv * hits
        return 0

    lax.fori_loop(0, bases, convolve_cols, 0, unroll=9)
    science = arrived_ref[pl.ds(group * VISITS, VISITS), 0:SUBS, :].reshape(per, LANES)
    weighted[PITCH * bases : PITCH * bases + per, :] = hits
    weighted[PITCH * columns : PITCH * columns + per, :] = science * hits

    def gram_of(b, _):
        flat = jnp.concatenate([weighted[pl.ds(SUBS * b + q, 32, stride=PITCH), :] for q in range(SUBS)], axis=1)
        high, low = split(flat)
        both = jnp.concatenate([high, low], axis=0)
        out = lax.dot_general(both, both, NT, preferred_element_type=F32)
        cross = out[0:32, 32:64] + out[32:64, 0:32]
        gram[b, :, 0:32] = cross + out[0:32, 0:32]
        return 0

    lax.fori_loop(0, VISITS, gram_of, 0, unroll=4)

    lane = iota((LANES, LANES), 1)
    groups = []
    for g in range(4):
        picked = [gram[:, 8 * g + jj, :] for jj in range(8)]
        stacked = jnp.concatenate(picked, axis=0)
        groups.append(stacked.T[0:32])
    lane = iota((32, LANES), 1)
    sub = iota((32, LANES), 0)
    for g in range(4):
        diagonal = (sub == 8 * g + lane // VISITS) & (sub < columns)
        groups[g] = groups[g] + jnp.where(diagonal, RIDGE, 0.0)
    visit = lane % VISITS
    for k in range(columns):
        factor = jnp.take_along_axis(groups[k // 8], visit + VISITS * (k % 8), axis=1)
        pivot = factor[k : k + 1, :]
        inverse = 1.0 / pivot
        scaled = jnp.where(sub == k, (pivot - 1.0) * inverse, factor * inverse)
        for g in range(k // 8, 4):
            groups[g] = groups[g] - scaled * groups[g][k : k + 1, :]
    target = columns
    answer = jnp.take_along_axis(groups[target // 8], lane // SUBS + VISITS * (target % 8), axis=1)
    coeff = jnp.concatenate([answer, jnp.zeros((LANES - 32, LANES), F32)], axis=0).T

    residual = science - coeff[:, bases : bases + 1]
    for k in range(bases):
        residual = residual - coeff[:, k : k + 1] * design[k]
    out_ref[pl.ds(group * VISITS, VISITS)] = residual.reshape(VISITS, SUBS, LANES)


def unpack_kernel(dest_ref, back_ref, out_ref, count):
    peers = back_ref.shape[0]
    strips = out_ref.shape[0]

    def clear(d, _):
        count[d] = 0
        return 0

    lax.fori_loop(0, peers, clear, 0, unroll=min(peers, 16))

    def pick(s, _):
        d = dest_ref[s]
        rank = count[d]
        count[d] = rank + 1
        both = back_ref[d]
        half = SUBS // CAP
        out_ref[s] = jnp.where(rank == 0, both[0:half], both[half:SUBS])
        return 0

    lax.fori_loop(0, strips, pick, 0, unroll=min(strips, 16))


VMEM = pl.BlockSpec(memory_space=pltpu.VMEM)
SMEM = pl.BlockSpec(memory_space=pltpu.SMEM)
HBM = pl.BlockSpec(memory_space=pltpu.HBM)


def on_device(
    template, science, dest, row_offset, col_block, basis_rows, basis_cols, stamp_rows, stamp_cols
):
    peers = lax.axis_size("patch")
    rows, cols = template.shape
    strips, strip_rows, block_cols = science.shape
    bases = basis_rows.shape[0]
    targets = dest.reshape(strips)
    last = cols // LANES - 1

    payload = pl.pallas_call(
        pack_kernel,
        grid=(1,),
        out_shape=jax.ShapeDtypeStruct((peers, 2 * SUBS, LANES), F32),
        in_specs=[
            SMEM, SMEM, SMEM,
            pl.BlockSpec((rows, LANES), lambda i: (0, 0)),
            pl.BlockSpec((rows, LANES), lambda i: (0, last)),
            VMEM,
        ],
        out_specs=VMEM,
        scratch_shapes=[pltpu.SMEM((peers,), jnp.int32), pltpu.SMEM((CAP * peers,), jnp.int32)],
        name="pack",
    )(targets, row_offset, col_block, template, template, science)

    arrived = lax.all_to_all(payload, "patch", split_axis=0, concat_axis=0, tiled=True)

    frame, col_taps, row_taps, mask = pl.pallas_call(
        prep_kernel,
        out_shape=(
            pltpu.VMEM((cols // LANES + 1, rows + 40, LANES), F32),
            pltpu.VMEM((bases, 2 * LANES, LANES), BF16),
            pltpu.VMEM((bases * SUBS, 2 * LANES), BF16),
            pltpu.VMEM((cols // LANES, rows + SUBS, LANES), F32),
        ),
        in_specs=[VMEM, VMEM, VMEM, VMEM, VMEM],
        out_specs=(VMEM, VMEM, VMEM, VMEM),
        scratch_shapes=[pltpu.VMEM((32, LANES), F32), pltpu.VMEM((LANES, LANES), F32)],
        name="prep",
    )(template, basis_rows.T, basis_cols.T, stamp_rows, stamp_cols)

    per = VISITS * SUBS
    residual = pl.pallas_call(
        main_kernel,
        in_specs=[VMEM, VMEM, VMEM, VMEM, VMEM],
        out_specs=VMEM,
        scratch_shapes=[
            pltpu.VMEM((cols // LANES + 1, rows + 40, LANES), F32),
            pltpu.VMEM((peers, LANES), F32),
            pltpu.SMEM((peers, LANES), F32),
            pltpu.VMEM((per, LANES), F32),
            pltpu.VMEM((bases, 2 * per, 2 * LANES), BF16),
            pltpu.VMEM((bases + 1, per, LANES), F32),
            pltpu.VMEM((32 * PITCH, LANES), F32),
            pltpu.VMEM((VISITS, 32, LANES), F32),
            pltpu.SemaphoreType.DMA,
        ],
        out_shape=jax.ShapeDtypeStruct((peers, SUBS, LANES), F32),
        compiler_params=pltpu.CompilerParams(vmem_limit_bytes=24 << 20),
        name="fit",
    )(arrived, frame, col_taps, row_taps, mask)

    returned = lax.all_to_all(residual, "patch", split_axis=0, concat_axis=0, tiled=True)

    return pl.pallas_call(
        unpack_kernel,
        out_shape=jax.ShapeDtypeStruct(science.shape, F32),
        in_specs=[SMEM, VMEM],
        out_specs=VMEM,
        scratch_shapes=[pltpu.SMEM((peers,), jnp.int32)],
        name="unpack",
    )(targets, returned)


def solution(mesh):
    placed = (
        P(None, ("groups", "patch")),
        P(("groups", "patch"), None, None),
        P(("groups", "patch"), None),
        P(("groups", "patch")),
        P(("groups", "patch")),
        P(),
        P(),
        P("groups", None),
        P("groups", None),
    )
    return jax.shard_map(
        on_device,
        mesh=mesh,
        in_specs=placed,
        out_specs=P(("groups", "patch"), None, None),
        check_vma=False,
    )
```

time: 52.5 us -> 37.9 us (0.72)
  Pallas kernels: 26.1 us -> 14.1 us
  waiting for transfers between devices: 0.9 us -> 5.81 us
  local copies, waits for them, and re-layouts: 4.76 us -> 0 us
  blocking collectives: 12.1 us -> 10.2 us
  other arithmetic: 0.59 us -> 0 us
    pallas_call x2, Pallas kernels: 22.7 us -> 10.9 us  [the longest x1 8.8 us: on_device(): pl.pallas_call(main_kernel, in_specs=[VMEM, VMEM, VMEM, VMEM, VMEM], out_...]
    all_to_all x1, waiting for transfers between devices: 0.9 us -> 5.81 us  [on_device(): lax.all_to_all(payload, 'patch', split_axis=0, concat_axis=0, tiled=True)]
    unnamed x5 -> x0, local copies, waits for them, and re-layouts: 4.76 us -> none
    all_to_all x1, blocking collectives: 12.1 us -> 10.2 us  [on_device(): lax.all_to_all(residual, 'patch', split_axis=0, concat_axis=0, tiled=True)]
    another operation x1 -> x0, other arithmetic: 0.59 us -> none  [on_device(): place = jnp.stack([own, jnp.int32(peers)])]
  transfers between devices with their start and end apart: 1 -> 1, of which waited for: 1 -> 1; matrix products, arithmetic and copies ran while one was open for 5% -> 0% of each run, Pallas kernels for 8% -> 6%
where the time goes in v2:
time: 37.9 us; the launch traced here: 37.6 us
  Pallas kernels  14.1 us (37%)
  blocking collectives  10.2 us (27%)
  starting transfers between devices  7.41 us (20%)
  waiting for transfers between devices  5.81 us (15%)
    all_to_all x1, blocking collectives, on_device(): lax.all_to_all(residual, 'patch', split_axis=0, concat_axis=0, tiled=True)  10.2 us
    pallas_call x1, Pallas kernels, on_device(): pl.pallas_call(main_kernel, in_specs=[VMEM, VMEM, VMEM, VMEM, VMEM], out_...  8.8 us
    all_to_all x1, starting transfers between devices, on_device(): lax.all_to_all(payload, 'patch', split_axis=0, concat_axis=0, tiled=True)  7.41 us
    all_to_all x1, waiting for transfers between devices, on_device(): lax.all_to_all(payload, 'patch', split_axis=0, concat_axis=0, tiled=True)  5.81 us
    pallas_call x1, Pallas kernels, on_device(): pl.pallas_call(prep_kernel, out_shape=(pltpu.VMEM((cols // LANES + 1, row...  2.08 us
    pallas_call x1, Pallas kernels, on_device(): pl.pallas_call(pack_kernel, grid=(1,), out_shape=jax.ShapeDtypeStruct((pe...  1.71 us
    pallas_call x1, Pallas kernels, on_device(): pl.pallas_call(unpack_kernel, out_shape=jax.ShapeDtypeStruct(science.shap...  1.55 us
  transfers between devices with their start and end apart: 1, of which 1 were waited for; matrix products, arithmetic and copies ran while one was open for 0% of the time, Pallas kernels for 6%

profile of v2, /device:TPU:0, one launch (start us, length us, event | category | flops | bytes accessed | tf_op | source)
XLA Modules:
  0.0 37.6 jit_solution(9971646372040196385)
XLA Ops:
  0.0 1.7 %pack.1 = f32[16,16,128]{2,1,0:T(8,128)} custom-call(s32[16]{0:T(128)} %bitcast.5, s32[16]{0:T(128)} %row_ref.1, s32[16]{0:T(128)} %col_ref.1, f32[64,1024]{1,0:T(8,128)} %template_ref.1, f32[64,1024]{1,0:T(8,128)} %template_ref.1, f32[16,4,128]{2,1,0:T(4,128)} %science_ref.1), custom_call_target="tpu_custom_call" | custom-call | tf_op jit(solution)/shard_map/pack/pallas_call | solution.py:319
  1.7 7.4 %all-to-all-start = ((f32[16,16,128]{2,1,0:T(8,128)}), f32[16,16,128]{2,1,0:T(8,128)S(1)}, u32[]{:S(2)}, u32[]{:S(2)}) async-start(f32[16,16,128]{2,1,0:T(8,128)} %pack.1), calls=%async_computation | async-start | bytes 262144 | tf_op jit(solution)/shard_map/all_to_all | solution.py:334
  9.1 2.1 %prep.1 = (f32[9,104,128]{2,1,0:T(8,128)S(1)}, bf16[27,256,128]{2,1,0:T(8,128)(2,1)S(1)}, bf16[216,256]{1,0:T(8,128)(2,1)S(1)}, f32[8,72,128]{2,1,0:T(8,128)S(1)}) custom-call(f32[64,1024]{1,0:T(8,128)} %template_ref.1, f32[21,27]{1,0:T(8,128)} %bitcast.3, f32[21,27]{1,0:T(8,128)} %bitcast.4, s32[16,24]{1,0:T(8,128)} %stamp_r_ref.1, s32[16,24]{1,0:T(8,128)} %stamp_c_ref.1), custom_call_target="tpu_custom_call" | custom-call | tf_op jit(solution)/shard_map/prep/pallas_call | solution.py:336
  11.2 5.8 %all-to-all-done.arrived_ref = f32[16,16,128]{2,1,0:T(8,128)S(1)} async-done(((f32[16,16,128]{2,1,0:T(8,128)}), f32[16,16,128]{2,1,0:T(8,128)S(1)}, u32[]{:S(2)}, u32[]{:S(2)}) %all-to-all-start) | async-done | bytes 131104 | tf_op jit(solution)/shard_map/all_to_all | solution.py:334
  17.0 8.8 %fit.1 = f32[16,8,128]{2,1,0:T(8,128)S(1)} custom-call(f32[16,16,128]{2,1,0:T(8,128)S(1)} %all-to-all-done.arrived_ref, f32[9,104,128]{2,1,0:T(8,128)S(1)} %get-tuple-element.9.frame_ref, bf16[27,256,128]{2,1,0:T(8,128)(2,1)S(1)} %get-tuple-element.10.col_taps_ref, bf16[216,256]{1,0:T(8,128)(2,1)S(1)} %get-tuple-element.11.row_taps_ref, ...), custom_call_target="tpu_custom_call" | custom-call | tf_op jit(solution)/shard_map/fit/pallas_call | solution.py:351
  25.8 10.2 %all_to_all.10.back_ref = f32[16,8,128]{2,1,0:T(8,128)} all-to-all(f32[16,8,128]{2,1,0:T(8,128)S(1)} %fit.1), channel_id=1, replica_groups=mesh['groups'=2,'patch'=16] {'patch'}, dimensions={0} | all-to-all | bytes 131072 | tf_op jit(solution)/shard_map/all_to_all | solution.py:371
  36.0 1.5 %unpack.1 = f32[16,4,128]{2,1,0:T(4,128)} custom-call(s32[16]{0:T(128)} %bitcast.6, f32[16,8,128]{2,1,0:T(8,128)} %all_to_all.10.back_ref), custom_call_target="tpu_custom_call" | custom-call | tf_op jit(solution)/shard_map/unpack/pallas_call | solution.py:373
Async XLA Ops:
  1.7 15.3 %all-to-all-start = ((f32[16,16,128]{2,1,0:T(8,128)}), f32[16,16,128]{2,1,0:T(8,128)S(1)}, u32[]{:S(2)}, u32[]{:S(2)}) async-start(f32[16,16,128]{2,1,0:T(8,128)} %pack.1), calls=%async_computation | async-start | bytes 262144 | tf_op jit(solution)/shard_map/all_to_all | solution.py:334

commit v3 on v2

--- a/solution.py
+++ b/solution.py
@@ -218,7 +218,7 @@
         field[:, pl.ds(per + at, 2 * SUBS), :] = low
         return 0
 
-    lax.fori_loop(0, VISITS // 2, convolve_rows, 0, unroll=2)
+    lax.fori_loop(0, VISITS // 2, convolve_rows, 0, unroll=VISITS // 2)
 
     hits = weight[...]
 
@@ -234,7 +234,7 @@
         weighted[pl.ds(PITCH * k, per), :] = conv * hits
         return 0
 
-    lax.fori_loop(0, bases, convolve_cols, 0, unroll=9)
+    lax.fori_loop(0, bases, convolve_cols, 0, unroll=bases)
     science = arrived_ref[pl.ds(group * VISITS, VISITS), 0:SUBS, :].reshape(per, LANES)
     weighted[PITCH * bases : PITCH * bases + per, :] = hits
     weighted[PITCH * columns : PITCH * columns + per, :] = science * hits
@@ -245,10 +245,10 @@
         both = jnp.concatenate([high, low], axis=0)
         out = lax.dot_general(both, both, NT, preferred_element_type=F32)
         cross = out[0:32, 32:64] + out[32:64, 0:32]
-        gram[b, :, 0:32] = cross + out[0:32, 0:32]
-        return 0
-
-    lax.fori_loop(0, VISITS, gram_of, 0, unroll=4)
+        gram[b, :, 0:32] = (out[32:64, 32:64] + cross) + out[0:32, 0:32]
+        return 0
+
+    lax.fori_loop(0, VISITS, gram_of, 0, unroll=8)
 
     lane = iota((LANES, LANES), 1)
     groups = []
@@ -262,15 +262,21 @@
         diagonal = (sub == 8 * g + lane // VISITS) & (sub < columns)
         groups[g] = groups[g] + jnp.where(diagonal, RIDGE, 0.0)
     visit = lane % VISITS
-    for k in range(columns):
-        factor = jnp.take_along_axis(groups[k // 8], visit + VISITS * (k % 8), axis=1)
-        pivot = factor[k : k + 1, :]
-        inverse = 1.0 / pivot
-        scaled = jnp.where(sub == k, (pivot - 1.0) * inverse, factor * inverse)
-        for g in range(k // 8, 4):
-            groups[g] = groups[g] - scaled * groups[g][k : k + 1, :]
-    target = columns
-    answer = jnp.take_along_axis(groups[target // 8], lane // SUBS + VISITS * (target % 8), axis=1)
+    scale = jnp.zeros((32, LANES), F32)
+    for p in range(4):
+        ends = min(8 * p + 8, columns + 1)
+        panel = {j: jnp.take_along_axis(groups[p], visit + VISITS * (j - 8 * p), axis=1) for j in range(8 * p, ends)}
+        for k in range(8 * p, min(ends, columns)):
+            here = sub == k
+            inverse = 1.0 / panel[k][k : k + 1, :]
+            scaled = jnp.where(here, 0.0, panel[k] * inverse)
+            scale = jnp.where(here, inverse, scale)
+            for j in range(k + 1, ends):
+                panel[j] = panel[j] - scaled * panel[j][k : k + 1, :]
+            for g in range(p + 1, 4):
+                groups[g] = groups[g] - scaled * groups[g][k : k + 1, :]
+    answer = panel[columns] * scale
+    answer = jnp.take_along_axis(answer, lane // SUBS, axis=1)
     coeff = jnp.concatenate([answer, jnp.zeros((LANES - 32, LANES), F32)], axis=0).T
 
     residual = science - coeff[:, bases : bases + 1]
@@ -319,7 +325,7 @@
     payload = pl.pallas_call(
         pack_kernel,
         grid=(1,),
-        out_shape=jax.ShapeDtypeStruct((peers, 2 * SUBS, LANES), F32),
+        out_shape=(pltpu.VMEM if peers <= VISITS else jax.ShapeDtypeStruct)((peers, 2 * SUBS, LANES), F32),
         in_specs=[
             SMEM, SMEM, SMEM,
             pl.BlockSpec((rows, LANES), lambda i: (0, 0)),
@@ -376,6 +382,7 @@
         in_specs=[SMEM, VMEM],
         out_specs=VMEM,
         scratch_shapes=[pltpu.SMEM((peers,), jnp.int32)],
+        compiler_params=pltpu.CompilerParams(vmem_limit_bytes=8 << 20),
         name="unpack",
     )(targets, returned)
 

time: 37.9 us -> 33.8 us (0.89)
  Pallas kernels: 14.1 us -> 10.6 us
  blocking collectives: 10.2 us -> 9.48 us
    pallas_call x1, Pallas kernels: 8.8 us -> 5.58 us  [on_device(): pl.pallas_call(main_kernel, in_specs=[VMEM, VMEM, VMEM, VMEM, VMEM], out_...]
    all_to_all x1, blocking collectives: 10.2 us -> 9.48 us  [on_device(): lax.all_to_all(residual, 'patch', split_axis=0, concat_axis=0, tiled=True)]
where the time goes in v3:
time: 33.8 us; the launch traced here: 33.5 us
  Pallas kernels  10.6 us (31%)
  blocking collectives  9.48 us (28%)
  starting transfers between devices  7.55 us (22%)
  waiting for transfers between devices  5.81 us (17%)
    all_to_all x1, blocking collectives, on_device(): lax.all_to_all(residual, 'patch', split_axis=0, concat_axis=0, tiled=True)  9.48 us
    all_to_all x1, starting transfers between devices, on_device(): lax.all_to_all(payload, 'patch', split_axis=0, concat_axis=0, tiled=True)  7.55 us
    all_to_all x1, waiting for transfers between devices, on_device(): lax.all_to_all(payload, 'patch', split_axis=0, concat_axis=0, tiled=True)  5.81 us
    pallas_call x1, Pallas kernels, on_device(): pl.pallas_call(main_kernel, in_specs=[VMEM, VMEM, VMEM, VMEM, VMEM], out_...  5.58 us
    pallas_call x1, Pallas kernels, on_device(): pl.pallas_call(prep_kernel, out_shape=(pltpu.VMEM((cols // LANES + 1, row...  2.09 us
    pallas_call x1, Pallas kernels, on_device(): pl.pallas_call(pack_kernel, grid=(1,), out_shape=(pltpu.VMEM if peers <=...  1.71 us
    pallas_call x1, Pallas kernels, on_device(): pl.pallas_call(unpack_kernel, out_shape=jax.ShapeDtypeStruct(science.shap...  1.24 us
  transfers between devices with their start and end apart: 1, of which 1 were waited for; matrix products, arithmetic and copies ran while one was open for 0% of the time, Pallas kernels for 6%

profile of v3, /device:TPU:0, one launch (start us, length us, event | category | flops | bytes accessed | tf_op | source)
XLA Modules:
  0.0 33.5 jit_solution(13109168803829006655)
XLA Ops:
  0.0 1.7 %pack.1 = f32[16,16,128]{2,1,0:T(8,128)} custom-call(s32[16]{0:T(128)} %bitcast.3, s32[16]{0:T(128)} %row_ref.1, s32[16]{0:T(128)} %col_ref.1, f32[64,1024]{1,0:T(8,128)} %template_ref.1, f32[64,1024]{1,0:T(8,128)} %template_ref.1, f32[16,4,128]{2,1,0:T(4,128)} %science_ref.1), custom_call_target="tpu_custom_call" | custom-call | tf_op jit(solution)/shard_map/pack/pallas_call | solution.py:325
  1.7 0.0 copy-start
  1.7 7.5 %all-to-all-start = ((f32[16,16,128]{2,1,0:T(8,128)}), f32[16,16,128]{2,1,0:T(8,128)S(1)}, u32[]{:S(2)}, u32[]{:S(2)}) async-start(f32[16,16,128]{2,1,0:T(8,128)} %pack.1), calls=%async_computation | async-start | bytes 262144 | tf_op jit(solution)/shard_map/all_to_all | solution.py:340
  9.3 2.1 %prep.1 = (f32[9,104,128]{2,1,0:T(8,128)S(1)}, bf16[27,256,128]{2,1,0:T(8,128)(2,1)S(1)}, bf16[216,256]{1,0:T(8,128)(2,1)S(1)}, f32[8,72,128]{2,1,0:T(8,128)S(1)}) custom-call(f32[64,1024]{1,0:T(8,128)} %template_ref.1, f32[21,27]{1,0:T(8,128)} %bitcast.5, f32[21,27]{1,0:T(8,128)} %bitcast.6, s32[16,24]{1,0:T(8,128)} %stamp_r_ref.1, s32[16,24]{1,0:T(8,128)} %stamp_c_ref.1), custom_call_target="tpu_custom_call" | custom-call | tf_op jit(solution)/shard_map/prep/pallas_call | solution.py:342
  11.4 5.8 %all-to-all-done.arrived_ref = f32[16,16,128]{2,1,0:T(8,128)S(1)} async-done(((f32[16,16,128]{2,1,0:T(8,128)}), f32[16,16,128]{2,1,0:T(8,128)S(1)}, u32[]{:S(2)}, u32[]{:S(2)}) %all-to-all-start) | async-done | bytes 131104 | tf_op jit(solution)/shard_map/all_to_all | solution.py:340
  17.2 5.6 %fit.1 = f32[16,8,128]{2,1,0:T(8,128)S(1)} custom-call(f32[16,16,128]{2,1,0:T(8,128)S(1)} %all-to-all-done.arrived_ref, f32[9,104,128]{2,1,0:T(8,128)S(1)} %get-tuple-element.9.frame_ref, bf16[27,256,128]{2,1,0:T(8,128)(2,1)S(1)} %get-tuple-element.10.col_taps_ref, bf16[216,256]{1,0:T(8,128)(2,1)S(1)} %get-tuple-element.11.row_taps_ref, ...), custom_call_target="tpu_custom_call" | custom-call | tf_op jit(solution)/shard_map/fit/pallas_call | solution.py:357
  22.8 9.5 %all_to_all.10.back_ref = f32[16,8,128]{2,1,0:T(8,128)S(1)} all-to-all(f32[16,8,128]{2,1,0:T(8,128)S(1)} %fit.1), channel_id=1, replica_groups=mesh['groups'=2,'patch'=16] {'patch'}, dimensions={0} | all-to-all | bytes 131072 | tf_op jit(solution)/shard_map/all_to_all | solution.py:377
  32.2 0.0 copy-done
  32.2 1.2 %unpack.1 = f32[16,4,128]{2,1,0:T(4,128)} custom-call(s32[16]{0:T(128)S(1)} %bitcast.4, f32[16,8,128]{2,1,0:T(8,128)S(1)} %all_to_all.10.back_ref), custom_call_target="tpu_custom_call" | custom-call | tf_op jit(solution)/shard_map/unpack/pallas_call | solution.py:379
Async XLA Ops:
  1.7 30.5 %copy-start = (s32[16,1]{0,1:T(1,128)S(1)}, s32[16,1]{0,1:T(1,128)}, u32[]{:S(2)}) copy-start(s32[16,1]{0,1:T(1,128)} %param.11) | copy-start | bytes 196
  1.7 15.5 %all-to-all-start = ((f32[16,16,128]{2,1,0:T(8,128)}), f32[16,16,128]{2,1,0:T(8,128)S(1)}, u32[]{:S(2)}, u32[]{:S(2)}) async-start(f32[16,16,128]{2,1,0:T(8,128)} %pack.1), calls=%async_computation | async-start | bytes 262144 | tf_op jit(solution)/shard_map/all_to_all | solution.py:340

commit v4 on v3

v4 whole, which is shorter than its diff:
```python
import jax
import jax.numpy as jnp
from jax import lax
from jax.experimental import pallas as pl
from jax.experimental.pallas import tpu as pltpu
from jax.sharding import PartitionSpec as P

CAP = 2
STAMP_HALF = 10
RIDGE = 1.0
LANES = 128
SUBS = 8
VISITS = 16
PITCH = VISITS * SUBS + 8

F32 = jnp.float32
BF16 = jnp.bfloat16
NT = (((1,), (1,)), ((), ()))


def iota(shape, dim):
    return lax.broadcasted_iota(jnp.int32, shape, dim)


def split(x):
    high = x.astype(BF16)
    return high, (x - high.astype(F32)).astype(BF16)


INFO_ROW = 2
SHIFT = 10
TOP = 16
HEIGHT = 40


def pack_kernel(
    dest_hbm, row_hbm, col_hbm, template_hbm, science_hbm, out_ref, slot_ref,
    dest_ref, row_ref, col_ref, edge, science_ref, count, source, sems,
):
    peers = out_ref.shape[0]
    strips = science_ref.shape[0]
    own = lax.axis_index("patch")
    rows = LANES // 2
    last = template_hbm.shape[1] - LANES
    copies = [
        pltpu.make_async_copy(source_ref, target_ref, sems.at[i])
        for i, (source_ref, target_ref) in enumerate(
            (
                (dest_hbm, dest_ref),
                (template_hbm.at[:, 0:LANES], edge.at[0:rows]),
                (template_hbm.at[:, last : last + LANES], edge.at[rows : 2 * rows]),
                (row_hbm, row_ref),
                (col_hbm, col_ref),
                (science_hbm, science_ref),
            )
        )
    ]
    for copy in copies:
        copy.start()

    def clear(d, _):
        count[d] = 0
        for r in range(CAP):
            source[CAP * d + r] = -1
        return 0

    lax.fori_loop(0, peers, clear, 0, unroll=min(peers, 16))

    def place(s, _):
        d = dest_ref[s]
        rank = count[d]
        source[CAP * d + rank] = s
        slot_ref[s] = CAP * d + rank
        count[d] = rank + 1
        return 0

    copies[0].wait()
    lax.fori_loop(0, strips, place, 0, unroll=min(strips, 16))
    for copy in copies[1:]:
        copy.wait()

    edges = edge[...].T
    lane = iota((SUBS, LANES), 1)
    sub = iota((SUBS, LANES), 0)
    low = lane < rows
    head = jnp.where(low, edges[0:8], pltpu.roll(edges[8:16], rows, 1))
    tail = jnp.where(low, pltpu.roll(edges[120:128], rows, 1), edges[112:120])
    info_here = (~low) & (sub == INFO_ROW)

    def fill(d, _):
        halo = jnp.where(d == own + 1, tail, head)
        info = jnp.zeros((SUBS, LANES), F32)
        parts = []
        for r in range(CAP):
            s = source[CAP * d + r]
            live = s >= 0
            at = jnp.maximum(s, 0)
            strip = science_ref[at]
            parts.append(jnp.where(live, strip, 0.0))
            values = (row_ref[at], col_ref[at], jnp.int32(1))
            for j, value in enumerate(values):
                value = jnp.where(live, value, 0).astype(F32)
                info = jnp.where(lane == rows + 3 * r + j, value, info)
        out_ref[d, 0:SUBS, :] = jnp.concatenate(parts, axis=0)
        out_ref[d, SUBS : 2 * SUBS, :] = jnp.where(info_here, info, halo)
        return 0

    lax.fori_loop(0, peers, fill, 0, unroll=min(peers, 16))


def prep_kernel(
    template_ref, rows_ref, cols_ref, stamp_r_ref, stamp_c_ref, frame_ref, col_taps_ref, row_taps_ref, mask_ref, pad_c, pad_t
):
    taps, bases = rows_ref.shape
    own = lax.axis_index("patch")
    rows = template_ref.shape[0]
    height = rows + HEIGHT
    blocks = frame_ref.shape[0] // height
    starts = iota((rows, LANES), 1) < SHIFT
    before = jnp.zeros((rows, LANES), F32)
    for c in range(blocks):
        here = jnp.zeros((rows, LANES), F32)
        if c < blocks - 1:
            here = pltpu.roll(template_ref[:, LANES * c : LANES * (c + 1)], SHIFT, 1)
        at = height * c
        frame_ref[at : at + TOP, :] = jnp.zeros((TOP, LANES), F32)
        frame_ref[at + TOP : at + TOP + rows, :] = jnp.where(starts, before, here)
        frame_ref[at + TOP + rows : at + height, :] = jnp.zeros((HEIGHT - TOP, LANES), F32)
        before = here
    sub_rows = rows
    blocks = blocks - 1
    sub_cols = blocks * LANES
    centre_r = stamp_r_ref[pl.ds(own, 1), :]
    centre_c = stamp_c_ref[pl.ds(own, 1), :]
    stamps = centre_r.shape[1]
    row_hit = (jnp.abs(iota((sub_rows, stamps), 0) - centre_r) <= STAMP_HALF).astype(F32).astype(BF16)
    col_hit = (jnp.abs(iota((sub_cols, stamps), 0) - centre_c) <= STAMP_HALF).astype(F32).astype(BF16)
    counts = lax.dot_general(row_hit, col_hit, NT, preferred_element_type=F32)
    for c in range(blocks):
        at = height * c
        mask_ref[at : at + height, :] = jnp.zeros((height, LANES), F32)
        mask_ref[at + TOP - SHIFT : at + TOP - SHIFT + rows, :] = jnp.minimum(counts[:, LANES * c : LANES * (c + 1)], 1.0)
    pad_t[...] = jnp.zeros_like(pad_t)
    pad_t[0:taps, 0:bases] = cols_ref[...]
    pad_t[32 : 32 + taps, 0:bases] = rows_ref[...]
    filters = pad_t[...].T
    pad_c[...] = jnp.where(iota((32, LANES), 1) < 32, filters[0:32], 0.0)
    full = jnp.where(iota((32, LANES), 1) < 32, pltpu.roll(filters[0:32], LANES - 32, 1), 0.0)
    high = full.astype(BF16).astype(F32)
    base = high + pltpu.roll(high, 32, 1) + pltpu.roll(full - high, 64, 1)
    wide = jnp.concatenate([base, jnp.zeros_like(base)], axis=1)
    lower = iota((SUBS, 2 * LANES), 0) < SUBS // CAP
    tiles = []
    for k in range(bases):
        row = jnp.broadcast_to(wide[k : k + 1, :], (SUBS, 2 * LANES))
        row = pltpu.roll(row, 0, 1, stride=1, stride_axis=0)
        row = jnp.where(lower, row, pltpu.roll(row, 96 - SUBS // CAP, 1))
        tiles.append(row)
    row_taps_ref[...] = jnp.concatenate(tiles, axis=0).astype(BF16)
    def column(k, _):
        ring = jnp.broadcast_to(pad_c[pl.ds(k, 1), :], (LANES, LANES))
        high, low = split(pltpu.roll(ring, 0, 1, stride=1, stride_axis=0))
        col_taps_ref[k, 0:LANES, :] = high
        col_taps_ref[k, LANES : 2 * LANES, :] = low
        return 0

    lax.fori_loop(0, bases, column, 0, unroll=9)


def main_kernel(
    arrived_ref, frame_ref, col_taps_ref, row_taps_ref, mask_ref, out_ref,
    frame, weight, field, design, pairs, gram,
):
    own = lax.axis_index("patch")
    peers = arrived_ref.shape[0]
    bases = col_taps_ref.shape[0]
    rows = LANES // 2
    last = frame.shape[0] - rows - HEIGHT
    per = VISITS * SUBS

    left = jnp.where(own > 0, arrived_ref[jnp.maximum(own - 1, 0), SUBS : 2 * SUBS, :], 0.0)
    right = jnp.where(own < peers - 1, arrived_ref[jnp.minimum(own + 1, peers - 1), SUBS : 2 * SUBS, :], 0.0)
    gap = jnp.zeros((LANES - 4 * SUBS, LANES), F32)
    halo = jnp.concatenate([pltpu.roll(right, 64, 1), right, gap, pltpu.roll(left, 64, 1), left], axis=0).T
    halo = pltpu.roll(halo, SHIFT, 1)
    starts = iota((rows, LANES), 1) < SHIFT
    frame[...] = frame_ref[...]
    first_rows = slice(TOP, TOP + rows)
    last_rows = slice(last + TOP, last + TOP + rows)
    frame[first_rows, :] = jnp.where(starts, halo[0:rows], frame_ref[first_rows, :])
    frame[last_rows, :] = jnp.where(starts, frame_ref[last_rows, :], halo[rows : 2 * rows])
    columns = bases + 1
    design[PITCH * bases : PITCH * bases + per, :] = jnp.ones((per, LANES), F32)
    design[PITCH * (columns + 1) :, :] = jnp.zeros((design.shape[0] - PITCH * (columns + 1), LANES), F32)

    def fit_group(group, _):
        fit_visits(
            group, arrived_ref, col_taps_ref, row_taps_ref, mask_ref, out_ref,
            frame, weight, field, design, pairs, gram,
        )
        return 0

    if peers == VISITS:
        fit_group(0, 0)
    else:
        lax.fori_loop(0, peers // VISITS, fit_group, 0)


def fit_visits(
    group, arrived_ref, col_taps_ref, row_taps_ref, mask_ref, out_ref,
    frame, weight, field, design, pairs, gram,
):
    bases = col_taps_ref.shape[0]
    columns = bases + 1
    per = VISITS * SUBS
    row_taps = row_taps_ref[:, 0:192]

    height = LANES // 2 + HEIGHT
    info = arrived_ref[pl.ds(group * VISITS, VISITS), SUBS + INFO_ROW, :]
    block = pltpu.roll(info, LANES - 1, 1)
    live = pltpu.roll(info, LANES - 2, 1)
    places = jnp.where(live > 0.0, block * height + info + (TOP - SHIFT), height - 32.0).astype(jnp.int32)

    for b in range(VISITS):
        terms = []
        masks = []
        for r in range(CAP):
            first = places[b, LANES // 2 + 3 * r]
            sides = [frame[pl.ds(first + height * side, 32), :] for side in range(2)]
            high, low = split(jnp.concatenate(sides, axis=1))
            terms += [high, low, high]
            masks.append(mask_ref[pl.ds(first, SUBS), :][0 : SUBS // CAP])
        at = slice(SUBS * b, SUBS * (b + 1))
        weight[at, :] = jnp.concatenate(masks, axis=0)
        across = jnp.dot(row_taps, jnp.concatenate(terms, axis=0), preferred_element_type=F32)
        for k in range(bases):
            field[k, at, :] = across[SUBS * k : SUBS * (k + 1)]

    turn = LANES - 32
    inside = iota((32, LANES), 1) >= iota((32, LANES), 0) + turn

    def convolve_cols(k, _):
        bands = []
        for term in range(2):
            ring = col_taps_ref[k, LANES * term : LANES * (term + 1), :]
            ends = ring[turn:]
            none = jnp.zeros_like(ends)
            here = jnp.concatenate([ring[0:turn], jnp.where(inside, ends, none)], axis=0)
            beyond = jnp.concatenate([jnp.zeros_like(ring[0:turn]), jnp.where(inside, none, ends)], axis=0)
            bands.append(jnp.concatenate([here, beyond], axis=1))
        both = jnp.concatenate(split(field[k]), axis=0)
        out = lax.dot_general(both, jnp.concatenate(bands, axis=0), NT, preferred_element_type=F32)
        conv = (out[0:per, LANES:] + out[per:, 0:LANES]) + out[0:per, 0:LANES]
        design[pl.ds(PITCH * k, per), :] = conv
        return 0

    lax.fori_loop(0, bases, convolve_cols, 0, unroll=bases)
    science = arrived_ref[pl.ds(group * VISITS, VISITS), 0:SUBS, :].reshape(per, LANES)
    design[PITCH * columns : PITCH * columns + per, :] = science

    def gram_of(b, _):
        left, right = [], []
        for q in range(SUBS):
            high, low = split(design[pl.ds(SUBS * b + q, 32, stride=PITCH), :])
            hit = jnp.broadcast_to(weight[pl.ds(SUBS * b + q, 1), :], (32, LANES)).astype(BF16)
            both = jnp.concatenate([high, low], axis=0)
            left.append(both * jnp.concatenate([hit, hit], axis=0))
            right.append(both)
            pairs[b, 32 * q : 32 * (q + 1), 0:LANES] = high
            pairs[b, 32 * q : 32 * (q + 1), LANES:] = low
        left = jnp.concatenate(left, axis=1)
        right = jnp.concatenate(right, axis=1)
        out = lax.dot_general(left, right, NT, preferred_element_type=F32)
        cross = out[0:32, 32:64] + out[32:64, 0:32]
        gram[b, :, 0:32] = (out[32:64, 32:64] + cross) + out[0:32, 0:32]
        return 0

    lax.fori_loop(0, VISITS, gram_of, 0, unroll=16)

    lane = iota((LANES, LANES), 1)
    groups = []
    for g in range(4):
        picked = [gram[:, 8 * g + jj, :] for jj in range(8)]
        stacked = jnp.concatenate(picked, axis=0)
        groups.append(stacked[:, 0:32].T)
    lane = iota((32, LANES), 1)
    sub = iota((32, LANES), 0)
    for g in range(4):
        diagonal = (sub == 8 * g + lane // VISITS) & (sub < columns)
        groups[g] = groups[g] + jnp.where(diagonal, RIDGE, 0.0)
    visit = lane % VISITS
    scale = jnp.zeros((32, LANES), F32)
    for p in range(4):
        ends = min(8 * p + 8, columns + 1)
        panel = {j: jnp.take_along_axis(groups[p], visit + VISITS * (j - 8 * p), axis=1) for j in range(8 * p, ends)}
        for k in range(8 * p, min(ends, columns)):
            here = sub == k
            inverse = 1.0 / panel[k][k : k + 1, :]
            scaled = jnp.where(here, 0.0, panel[k] * inverse)
            scale = jnp.where(here, inverse, scale)
            for j in range(k + 1, ends):
                panel[j] = panel[j] - scaled * panel[j][k : k + 1, :]
            for g in range(p + 1, 4):
                groups[g] = groups[g] - scaled * groups[g][k : k + 1, :]
    answer = panel[columns] * scale
    answer = jnp.take_along_axis(answer, lane // SUBS, axis=1)
    coeff = jnp.concatenate([answer, jnp.zeros((LANES - 32, LANES), F32)], axis=0).T

    tiled = coeff + pltpu.roll(coeff, 32, 1)
    tiled = tiled + pltpu.roll(tiled, 64, 1)
    row = iota((SUBS, LANES), 0)
    side = iota((SUBS, LANES), 1) // 32
    for b in range(VISITS):
        own_rows = tiled[SUBS * b : SUBS * (b + 1)]
        spread = jnp.concatenate([jnp.where(side == row, own_rows, 0.0), jnp.where(side + 4 == row, own_rows, 0.0)], axis=1)
        high = spread.astype(BF16).astype(F32)
        terms = jnp.concatenate([high, spread - high], axis=0).astype(BF16)
        out = lax.dot_general(terms, pairs[b], (((1,), (0,)), ((), ())), preferred_element_type=F32)
        model = (out[0:SUBS, LANES:] + out[SUBS:, 0:LANES]) + out[0:SUBS, 0:LANES]
        out_ref[group * VISITS + b] = science[SUBS * b : SUBS * (b + 1)] - model


def unpack_kernel(slot_ref, back_ref, out_ref):
    strips = out_ref.shape[0]
    half = SUBS // CAP

    def pick(s, _):
        slot = slot_ref[s]
        both = back_ref[slot // CAP]
        out_ref[s] = jnp.where(slot % CAP == 0, both[0:half], both[half:SUBS])
        return 0

    lax.fori_loop(0, strips, pick, 0, unroll=min(strips, 16))


VMEM = pl.BlockSpec(memory_space=pltpu.VMEM)
SMEM = pl.BlockSpec(memory_space=pltpu.SMEM)
ANY = pl.BlockSpec(memory_space=pl.ANY)


def on_device(
    template, science, dest, row_offset, col_block, basis_rows, basis_cols, stamp_rows, stamp_cols
):
    peers = lax.axis_size("patch")
    rows, cols = template.shape
    strips, strip_rows, block_cols = science.shape
    bases = basis_rows.shape[0]
    blocks = cols // LANES
    height = rows + HEIGHT
    targets = dest.reshape(strips)

    kept = pltpu.VMEM if peers <= VISITS else jax.ShapeDtypeStruct
    payload, slots = pl.pallas_call(
        pack_kernel,
        out_shape=(kept((peers, 2 * SUBS, LANES), F32), pltpu.SMEM((strips,), jnp.int32)),
        in_specs=[ANY, ANY, ANY, ANY, ANY],
        out_specs=(VMEM, SMEM),
        scratch_shapes=[
            pltpu.SMEM((strips,), jnp.int32),
            pltpu.SMEM((strips,), jnp.int32),
            pltpu.SMEM((strips,), jnp.int32),
            pltpu.VMEM((2 * rows, LANES), F32),
            pltpu.VMEM((strips, strip_rows, block_cols), F32),
            pltpu.SMEM((peers,), jnp.int32),
            pltpu.SMEM((CAP * peers,), jnp.int32),
            pltpu.SemaphoreType.DMA((6,)),
        ],
        name="pack",
    )(targets, row_offset, col_block, template, science)

    arrived = lax.all_to_all(payload, "patch", split_axis=0, concat_axis=0, tiled=True)

    frame, col_taps, row_taps, mask = pl.pallas_call(
        prep_kernel,
        out_shape=(
            pltpu.VMEM(((blocks + 1) * height, LANES), F32),
            pltpu.VMEM((bases, 2 * LANES, LANES), BF16),
            pltpu.VMEM((bases * SUBS, 2 * LANES), BF16),
            pltpu.VMEM((blocks * height, LANES), F32),
        ),
        in_specs=[VMEM, VMEM, VMEM, VMEM, VMEM],
        out_specs=(VMEM, VMEM, VMEM, VMEM),
        scratch_shapes=[pltpu.VMEM((32, LANES), F32), pltpu.VMEM((LANES, LANES), F32)],
        name="prep",
    )(template, basis_rows.T, basis_cols.T, stamp_rows, stamp_cols)

    per = VISITS * SUBS
    residual = pl.pallas_call(
        main_kernel,
        in_specs=[VMEM, VMEM, VMEM, VMEM, VMEM],
        out_specs=VMEM,
        scratch_shapes=[
            pltpu.VMEM(((blocks + 1) * height, LANES), F32),
            pltpu.VMEM((per, LANES), F32),
            pltpu.VMEM((bases, per, 2 * LANES), F32),
            pltpu.VMEM((32 * PITCH, LANES), F32),
            pltpu.VMEM((VISITS, 2 * LANES, 2 * LANES), BF16),
            pltpu.VMEM((VISITS, 32, LANES), F32),
        ],
        out_shape=jax.ShapeDtypeStruct((peers, SUBS, LANES), F32),
        compiler_params=pltpu.CompilerParams(vmem_limit_bytes=24 << 20),
        name="fit",
    )(arrived, frame, col_taps, row_taps, mask)

    returned = lax.all_to_all(residual, "patch", split_axis=0, concat_axis=0, tiled=True)

    return pl.pallas_call(
        unpack_kernel,
        out_shape=jax.ShapeDtypeStruct(science.shape, F32),
        in_specs=[SMEM, VMEM],
        out_specs=VMEM,
        compiler_params=pltpu.CompilerParams(vmem_limit_bytes=8 << 20),
        name="unpack",
    )(slots, returned)


def solution(mesh):
    placed = (
        P(None, ("groups", "patch")),
        P(("groups", "patch"), None, None),
        P(("groups", "patch"), None),
        P(("groups", "patch")),
        P(("groups", "patch")),
        P(),
        P(),
        P("groups", None),
        P("groups", None),
    )
    return jax.shard_map(
        on_device,
        mesh=mesh,
        in_specs=placed,
        out_specs=P(("groups", "patch"), None, None),
        check_vma=False,
    )
```

time: 33.8 us -> 32.1 us (0.950)
  Pallas kernels: 10.6 us -> 9.06 us
    pallas_call x1, Pallas kernels: 5.58 us -> 4.54 us  [on_device(): pl.pallas_call(main_kernel, in_specs=[VMEM, VMEM, VMEM, VMEM, VMEM], out_...]
    pallas_call x1, Pallas kernels: 1.24 us -> 0.71 us  [on_device(): pl.pallas_call(unpack_kernel, out_shape=jax.ShapeDtypeStruct(science.shap...]
  transfers between devices with their start and end apart: 1 -> 1, of which waited for: 1 -> 1; matrix products, arithmetic and copies ran while one was open for 0% -> 0% of each run, Pallas kernels for 6% -> 7%
where the time goes in v4:
time: 32.1 us; the launch traced here: 31.8 us
  blocking collectives  9.48 us (30%)
  Pallas kernels  9.06 us (28%)
  starting transfers between devices  7.43 us (23%)
  waiting for transfers between devices  5.79 us (18%)
    all_to_all x1, blocking collectives, on_device(): lax.all_to_all(residual, 'patch', split_axis=0, concat_axis=0, tiled=True)  9.48 us
    all_to_all x1, starting transfers between devices, on_device(): lax.all_to_all(payload, 'patch', split_axis=0, concat_axis=0, tiled=True)  7.43 us
    all_to_all x1, waiting for transfers between devices, on_device(): lax.all_to_all(payload, 'patch', split_axis=0, concat_axis=0, tiled=True)  5.79 us
    pallas_call x1, Pallas kernels, on_device(): pl.pallas_call(main_kernel, in_specs=[VMEM, VMEM, VMEM, VMEM, VMEM], out_...  4.54 us
    pallas_call x1, Pallas kernels, on_device(): pl.pallas_call(prep_kernel, out_shape=(pltpu.VMEM(((blocks + 1) * height,...  2.11 us
    pallas_call x1, Pallas kernels, on_device(): pl.pallas_call(pack_kernel, out_shape=(kept((peers, 2 * SUBS, LANES), F32...  1.7 us
    pallas_call x1, Pallas kernels, on_device(): pl.pallas_call(unpack_kernel, out_shape=jax.ShapeDtypeStruct(science.shap...  0.71 us
  transfers between devices with their start and end apart: 1, of which 1 were waited for; matrix products, arithmetic and copies ran while one was open for 0% of the time, Pallas kernels for 7%

profile of v4, /device:TPU:0, one launch (start us, length us, event | category | flops | bytes accessed | tf_op | source)
XLA Modules:
  0.0 31.8 jit_solution(17392550769002892577)
XLA Ops:
  0.0 1.7 %pack.1 = (f32[16,16,128]{2,1,0:T(8,128)}, s32[16]{0:T(128)S(4)}) custom-call(s32[16]{0:T(128)} %bitcast.5, s32[16]{0:T(128)} %row_hbm.1, s32[16]{0:T(128)} %col_hbm.1, f32[64,1024]{1,0:T(8,128)} %template_ref.1, f32[16,4,128]{2,1,0:T(4,128)} %science_hbm.1), custom_call_target="tpu_custom_call" | custom-call | tf_op jit(solution)/shard_map/pack/pallas_call | solution.py:353
  1.7 7.4 %all-to-all-start = ((f32[16,16,128]{2,1,0:T(8,128)}), f32[16,16,128]{2,1,0:T(8,128)S(1)}, u32[]{:S(2)}, u32[]{:S(2)}) async-start(f32[16,16,128]{2,1,0:T(8,128)} %get-tuple-element.12), calls=%async_computation | async-start | bytes 262144 | tf_op jit(solution)/shard_map/all_to_all | solution.py:371
  9.1 2.1 %prep.1 = (f32[936,128]{1,0:T(8,128)S(1)}, bf16[27,256,128]{2,1,0:T(8,128)(2,1)S(1)}, bf16[216,256]{1,0:T(8,128)(2,1)S(1)}, f32[832,128]{1,0:T(8,128)S(1)}) custom-call(f32[64,1024]{1,0:T(8,128)} %template_ref.1, f32[21,27]{1,0:T(8,128)} %bitcast.3, f32[21,27]{1,0:T(8,128)} %bitcast.4, s32[16,24]{1,0:T(8,128)} %stamp_r_ref.1, s32[16,24]{1,0:T(8,128)} %stamp_c_ref.1), custom_call_target="tpu_custom_call" | custom-call | tf_op jit(solution)/shard_map/prep/pallas_call | solution.py:373
  11.3 5.8 %all-to-all-done.arrived_ref = f32[16,16,128]{2,1,0:T(8,128)S(1)} async-done(((f32[16,16,128]{2,1,0:T(8,128)}), f32[16,16,128]{2,1,0:T(8,128)S(1)}, u32[]{:S(2)}, u32[]{:S(2)}) %all-to-all-start) | async-done | bytes 131104 | tf_op jit(solution)/shard_map/all_to_all | solution.py:371
  17.0 4.5 %fit.1 = f32[16,8,128]{2,1,0:T(8,128)S(1)} custom-call(f32[16,16,128]{2,1,0:T(8,128)S(1)} %all-to-all-done.arrived_ref, f32[936,128]{1,0:T(8,128)S(1)} %get-tuple-element.13.frame_ref, bf16[27,256,128]{2,1,0:T(8,128)(2,1)S(1)} %get-tuple-element.14.col_taps_ref, bf16[216,256]{1,0:T(8,128)(2,1)S(1)} %get-tuple-element.15.row_taps_ref, ...), custom_call_target="tpu_custom_call" | custom-call | tf_op jit(solution)/shard_map/fit/pallas_call | solution.py:388
  21.6 9.5 %all_to_all.10.back_ref = f32[16,8,128]{2,1,0:T(8,128)S(1)} all-to-all(f32[16,8,128]{2,1,0:T(8,128)S(1)} %fit.1), channel_id=1, replica_groups=mesh['groups'=2,'patch'=16] {'patch'}, dimensions={0} | all-to-all | bytes 131072 | tf_op jit(solution)/shard_map/all_to_all | solution.py:405
  31.1 0.7 %unpack.1 = f32[16,4,128]{2,1,0:T(4,128)} custom-call(s32[16]{0:T(128)S(4)} %get-tuple-element.11.slot_ref, f32[16,8,128]{2,1,0:T(8,128)S(1)} %all_to_all.10.back_ref), custom_call_target="tpu_custom_call" | custom-call | tf_op jit(solution)/shard_map/unpack/pallas_call | solution.py:407
Async XLA Ops:
  1.7 15.3 %all-to-all-start = ((f32[16,16,128]{2,1,0:T(8,128)}), f32[16,16,128]{2,1,0:T(8,128)S(1)}, u32[]{:S(2)}, u32[]{:S(2)}) async-start(f32[16,16,128]{2,1,0:T(8,128)} %get-tuple-element.12), calls=%async_computation | async-start | bytes 262144 | tf_op jit(solution)/shard_map/all_to_all | solution.py:371

commit v5 on v4

--- a/solution.py
+++ b/solution.py
@@ -30,6 +30,7 @@
 INFO_ROW = 2
 SHIFT = 10
 TOP = 16
+AHEAD = 4
 HEIGHT = 40
 
 
@@ -168,8 +169,8 @@
 
 
 def main_kernel(
-    arrived_ref, frame_ref, col_taps_ref, row_taps_ref, mask_ref, out_ref,
-    frame, weight, field, design, pairs, gram,
+    arrived_ref, frame_ref, col_taps_ref, row_taps_ref, mask_ref, out_ref, frame,
+    weight, field, design, pairs, gram,
 ):
     own = lax.axis_index("patch")
     peers = arrived_ref.shape[0]
@@ -184,14 +185,10 @@
     halo = jnp.concatenate([pltpu.roll(right, 64, 1), right, gap, pltpu.roll(left, 64, 1), left], axis=0).T
     halo = pltpu.roll(halo, SHIFT, 1)
     starts = iota((rows, LANES), 1) < SHIFT
-    frame[...] = frame_ref[...]
     first_rows = slice(TOP, TOP + rows)
     last_rows = slice(last + TOP, last + TOP + rows)
     frame[first_rows, :] = jnp.where(starts, halo[0:rows], frame_ref[first_rows, :])
     frame[last_rows, :] = jnp.where(starts, frame_ref[last_rows, :], halo[rows : 2 * rows])
-    columns = bases + 1
-    design[PITCH * bases : PITCH * bases + per, :] = jnp.ones((per, LANES), F32)
-    design[PITCH * (columns + 1) :, :] = jnp.zeros((design.shape[0] - PITCH * (columns + 1), LANES), F32)
 
     def fit_group(group, _):
         fit_visits(
@@ -256,62 +253,65 @@
 
     lax.fori_loop(0, bases, convolve_cols, 0, unroll=bases)
     science = arrived_ref[pl.ds(group * VISITS, VISITS), 0:SUBS, :].reshape(per, LANES)
+    design[PITCH * bases : PITCH * bases + per, :] = jnp.ones((per, LANES), F32)
     design[PITCH * columns : PITCH * columns + per, :] = science
+    design[PITCH * (columns + 1) :, :] = jnp.zeros((design.shape[0] - PITCH * (columns + 1), LANES), F32)
 
     def gram_of(b, _):
         left, right = [], []
         for q in range(SUBS):
             high, low = split(design[pl.ds(SUBS * b + q, 32, stride=PITCH), :])
-            hit = jnp.broadcast_to(weight[pl.ds(SUBS * b + q, 1), :], (32, LANES)).astype(BF16)
+            hit = jnp.broadcast_to(weight[pl.ds(SUBS * b + q, 1), :], (2 * SUBS, LANES)).astype(BF16)
             both = jnp.concatenate([high, low], axis=0)
-            left.append(both * jnp.concatenate([hit, hit], axis=0))
+            left.append(jnp.concatenate([both[16 * i : 16 * (i + 1)] * hit for i in range(4)], axis=0))
             right.append(both)
             pairs[b, 32 * q : 32 * (q + 1), 0:LANES] = high
             pairs[b, 32 * q : 32 * (q + 1), LANES:] = low
         left = jnp.concatenate(left, axis=1)
         right = jnp.concatenate(right, axis=1)
         out = lax.dot_general(left, right, NT, preferred_element_type=F32)
-        cross = out[0:32, 32:64] + out[32:64, 0:32]
-        gram[b, :, 0:32] = (out[32:64, 32:64] + cross) + out[0:32, 0:32]
-        return 0
-
-    lax.fori_loop(0, VISITS, gram_of, 0, unroll=16)
-
-    lane = iota((LANES, LANES), 1)
-    groups = []
-    for g in range(4):
-        picked = [gram[:, 8 * g + jj, :] for jj in range(8)]
-        stacked = jnp.concatenate(picked, axis=0)
-        groups.append(stacked[:, 0:32].T)
+        halves = out[32:64] + out[0:32]
+        gram[pl.ds(b, 32, stride=VISITS), :] = jnp.concatenate([halves, jnp.zeros((32, LANES - 64), F32)], axis=1)
+        return 0
+
+    lax.fori_loop(0, VISITS, gram_of, 0, unroll=VISITS)
+
+    groups = [gram[per * g : per * (g + 1), :].T for g in range(4)]
+    groups = [group[0:32] + group[32:64] for group in groups]
     lane = iota((32, LANES), 1)
     sub = iota((32, LANES), 0)
     for g in range(4):
         diagonal = (sub == 8 * g + lane // VISITS) & (sub < columns)
         groups[g] = groups[g] + jnp.where(diagonal, RIDGE, 0.0)
     visit = lane % VISITS
+
+    def spread(p):
+        ends = min(SUBS * (p + 1), columns + 1)
+        return {j: jnp.take_along_axis(groups[p], visit + VISITS * (j - SUBS * p), axis=1) for j in range(SUBS * p, ends)}
+
     scale = jnp.zeros((32, LANES), F32)
-    for p in range(4):
-        ends = min(8 * p + 8, columns + 1)
-        panel = {j: jnp.take_along_axis(groups[p], visit + VISITS * (j - 8 * p), axis=1) for j in range(8 * p, ends)}
-        for k in range(8 * p, min(ends, columns)):
-            here = sub == k
-            inverse = 1.0 / panel[k][k : k + 1, :]
-            scaled = jnp.where(here, 0.0, panel[k] * inverse)
-            scale = jnp.where(here, inverse, scale)
-            for j in range(k + 1, ends):
-                panel[j] = panel[j] - scaled * panel[j][k : k + 1, :]
-            for g in range(p + 1, 4):
+    panel = spread(0)
+    for k in range(columns):
+        p = k // SUBS
+        if k % SUBS == SUBS - AHEAD and p < 3:
+            panel.update(spread(p + 1))
+        here = sub == k
+        column = panel.pop(k)
+        inverse = 1.0 / column[k : k + 1, :]
+        scaled = jnp.where(here, 0.0, column * inverse)
+        scale = jnp.where(here, inverse, scale)
+        for j in panel:
+            panel[j] = panel[j] - scaled * panel[j][k : k + 1, :]
+        for g in range(p + 1, 4):
+            if SUBS * g not in panel:
                 groups[g] = groups[g] - scaled * groups[g][k : k + 1, :]
     answer = panel[columns] * scale
-    answer = jnp.take_along_axis(answer, lane // SUBS, axis=1)
-    coeff = jnp.concatenate([answer, jnp.zeros((LANES - 32, LANES), F32)], axis=0).T
-
-    tiled = coeff + pltpu.roll(coeff, 32, 1)
-    tiled = tiled + pltpu.roll(tiled, 64, 1)
+    tiled = jnp.concatenate([answer] * 4, axis=0).T
+
     row = iota((SUBS, LANES), 0)
     side = iota((SUBS, LANES), 1) // 32
     for b in range(VISITS):
-        own_rows = tiled[SUBS * b : SUBS * (b + 1)]
+        own_rows = jnp.broadcast_to(tiled[b : b + 1], (SUBS, LANES))
         spread = jnp.concatenate([jnp.where(side == row, own_rows, 0.0), jnp.where(side + 4 == row, own_rows, 0.0)], axis=1)
         high = spread.astype(BF16).astype(F32)
         terms = jnp.concatenate([high, spread - high], axis=0).astype(BF16)
@@ -385,19 +385,19 @@
     )(template, basis_rows.T, basis_cols.T, stamp_rows, stamp_cols)
 
     per = VISITS * SUBS
-    residual = pl.pallas_call(
+    residual, _ = pl.pallas_call(
         main_kernel,
         in_specs=[VMEM, VMEM, VMEM, VMEM, VMEM],
-        out_specs=VMEM,
+        out_specs=(VMEM, VMEM),
         scratch_shapes=[
-            pltpu.VMEM(((blocks + 1) * height, LANES), F32),
             pltpu.VMEM((per, LANES), F32),
             pltpu.VMEM((bases, per, 2 * LANES), F32),
             pltpu.VMEM((32 * PITCH, LANES), F32),
             pltpu.VMEM((VISITS, 2 * LANES, 2 * LANES), BF16),
-            pltpu.VMEM((VISITS, 32, LANES), F32),
+            pltpu.VMEM((VISITS * 32, LANES), F32),
         ],
-        out_shape=jax.ShapeDtypeStruct((peers, SUBS, LANES), F32),
+        out_shape=(jax.ShapeDtypeStruct((peers, SUBS, LANES), F32), pltpu.VMEM(((blocks + 1) * height, LANES), F32)),
+        input_output_aliases={1: 1},
         compiler_params=pltpu.CompilerParams(vmem_limit_bytes=24 << 20),
         name="fit",
     )(arrived, frame, col_taps, row_taps, mask)

time: 32.1 us -> 31.5 us (0.981)
  Pallas kernels: 9.06 us -> 8.5 us
    pallas_call x1, Pallas kernels: 4.54 us -> 3.97 us  [on_device(): pl.pallas_call(main_kernel, in_specs=[VMEM, VMEM, VMEM, VMEM, VMEM], out_...]
where the time goes in v5:
time: 31.5 us; the launch traced here: 31.2 us
  blocking collectives  9.49 us (30%)
  Pallas kernels  8.5 us (27%)
  starting transfers between devices  7.43 us (24%)
  waiting for transfers between devices  5.79 us (18%)
    all_to_all x1, blocking collectives, on_device(): lax.all_to_all(residual, 'patch', split_axis=0, concat_axis=0, tiled=True)  9.49 us
    all_to_all x1, starting transfers between devices, on_device(): lax.all_to_all(payload, 'patch', split_axis=0, concat_axis=0, tiled=True)  7.43 us
    all_to_all x1, waiting for transfers between devices, on_device(): lax.all_to_all(payload, 'patch', split_axis=0, concat_axis=0, tiled=True)  5.79 us
    pallas_call x1, Pallas kernels, on_device(): pl.pallas_call(main_kernel, in_specs=[VMEM, VMEM, VMEM, VMEM, VMEM], out_...  3.97 us
    pallas_call x1, Pallas kernels, on_device(): pl.pallas_call(prep_kernel, out_shape=(pltpu.VMEM(((blocks + 1) * height,...  2.11 us
    pallas_call x1, Pallas kernels, on_device(): pl.pallas_call(pack_kernel, out_shape=(kept((peers, 2 * SUBS, LANES), F32...  1.71 us
    pallas_call x1, Pallas kernels, on_device(): pl.pallas_call(unpack_kernel, out_shape=jax.ShapeDtypeStruct(science.shap...  0.71 us
  transfers between devices with their start and end apart: 1, of which 1 were waited for; matrix products, arithmetic and copies ran while one was open for 0% of the time, Pallas kernels for 7%

profile of v5, /device:TPU:0, one launch (start us, length us, event | category | flops | bytes accessed | tf_op | source)
XLA Modules:
  0.0 31.2 jit_solution(18324827639936557679)
XLA Ops:
  0.0 1.7 %pack.1 = (f32[16,16,128]{2,1,0:T(8,128)}, s32[16]{0:T(128)S(4)}) custom-call(s32[16]{0:T(128)} %bitcast.5, s32[16]{0:T(128)} %row_hbm.1, s32[16]{0:T(128)} %col_hbm.1, f32[64,1024]{1,0:T(8,128)} %template_ref.1, f32[16,4,128]{2,1,0:T(4,128)} %science_hbm.1), custom_call_target="tpu_custom_call" | custom-call | tf_op jit(solution)/shard_map/pack/pallas_call | solution.py:353
  1.7 7.4 %all-to-all-start = ((f32[16,16,128]{2,1,0:T(8,128)}), f32[16,16,128]{2,1,0:T(8,128)S(1)}, u32[]{:S(2)}, u32[]{:S(2)}) async-start(f32[16,16,128]{2,1,0:T(8,128)} %get-tuple-element.13), calls=%async_computation | async-start | bytes 262144 | tf_op jit(solution)/shard_map/all_to_all | solution.py:371
  9.2 2.1 %prep.1 = (f32[936,128]{1,0:T(8,128)S(1)}, bf16[27,256,128]{2,1,0:T(8,128)(2,1)S(1)}, bf16[216,256]{1,0:T(8,128)(2,1)S(1)}, f32[832,128]{1,0:T(8,128)S(1)}) custom-call(f32[64,1024]{1,0:T(8,128)} %template_ref.1, f32[21,27]{1,0:T(8,128)} %bitcast.3, f32[21,27]{1,0:T(8,128)} %bitcast.4, s32[16,24]{1,0:T(8,128)} %stamp_r_ref.1, s32[16,24]{1,0:T(8,128)} %stamp_c_ref.1), custom_call_target="tpu_custom_call" | custom-call | tf_op jit(solution)/shard_map/prep/pallas_call | solution.py:373
  11.3 5.8 %all-to-all-done.arrived_ref = f32[16,16,128]{2,1,0:T(8,128)S(1)} async-done(((f32[16,16,128]{2,1,0:T(8,128)}), f32[16,16,128]{2,1,0:T(8,128)S(1)}, u32[]{:S(2)}, u32[]{:S(2)}) %all-to-all-start) | async-done | bytes 131104 | tf_op jit(solution)/shard_map/all_to_all | solution.py:371
  17.1 4.0 %fit.1 = (f32[16,8,128]{2,1,0:T(8,128)S(1)}, f32[936,128]{1,0:T(8,128)S(1)}) custom-call(f32[16,16,128]{2,1,0:T(8,128)S(1)} %all-to-all-done.arrived_ref, f32[936,128]{1,0:T(8,128)S(1)} %get-tuple-element.14.frame_ref, bf16[27,256,128]{2,1,0:T(8,128)(2,1)S(1)} %get-tuple-element.15.col_taps_ref, ...), custom_call_target="tpu_custom_call", output_to_operand_aliasing={{1}: (1, {})} | custom-call | tf_op jit(solution)/shard_map/fit/pallas_call | solution.py:388
  21.0 9.5 %all_to_all.10.back_ref = f32[16,8,128]{2,1,0:T(8,128)S(1)} all-to-all(f32[16,8,128]{2,1,0:T(8,128)S(1)} %get-tuple-element.18), channel_id=1, replica_groups=mesh['groups'=2,'patch'=16] {'patch'}, dimensions={0} | all-to-all | bytes 131072 | tf_op jit(solution)/shard_map/all_to_all | solution.py:405
  30.5 0.7 %unpack.1 = f32[16,4,128]{2,1,0:T(4,128)} custom-call(s32[16]{0:T(128)S(4)} %get-tuple-element.12.slot_ref, f32[16,8,128]{2,1,0:T(8,128)S(1)} %all_to_all.10.back_ref), custom_call_target="tpu_custom_call" | custom-call | tf_op jit(solution)/shard_map/unpack/pallas_call | solution.py:407
Async XLA Ops:
  1.7 15.3 %all-to-all-start = ((f32[16,16,128]{2,1,0:T(8,128)}), f32[16,16,128]{2,1,0:T(8,128)S(1)}, u32[]{:S(2)}, u32[]{:S(2)}) async-start(f32[16,16,128]{2,1,0:T(8,128)} %get-tuple-element.13), calls=%async_computation | async-start | bytes 262144 | tf_op jit(solution)/shard_map/all_to_all | solution.py:371

commit v6 on v5

--- a/solution.py
+++ b/solution.py
@@ -27,7 +27,7 @@
     return high, (x - high.astype(F32)).astype(BF16)
 
 
-INFO_ROW = 2
+PARCEL = 14
 SHIFT = 10
 TOP = 16
 AHEAD = 4
@@ -38,7 +38,7 @@
     dest_hbm, row_hbm, col_hbm, template_hbm, science_hbm, out_ref, slot_ref,
     dest_ref, row_ref, col_ref, edge, science_ref, count, source, sems,
 ):
-    peers = out_ref.shape[0]
+    peers = out_ref.shape[0] // PARCEL
     strips = science_ref.shape[0]
     own = lax.axis_index("patch")
     rows = LANES // 2
@@ -84,9 +84,9 @@
     lane = iota((SUBS, LANES), 1)
     sub = iota((SUBS, LANES), 0)
     low = lane < rows
-    head = jnp.where(low, edges[0:8], pltpu.roll(edges[8:16], rows, 1))
-    tail = jnp.where(low, pltpu.roll(edges[120:128], rows, 1), edges[112:120])
-    info_here = (~low) & (sub == INFO_ROW)
+    head = jnp.where(low, edges[0:8], pltpu.roll(edges[5:13], rows, 1))
+    tail = jnp.where(low, pltpu.roll(edges[118:126], rows, 1), jnp.concatenate([edges[123:128], edges[0:3]], axis=0))
+    info_here = sub == PARCEL - 1 - SUBS
 
     def fill(d, _):
         halo = jnp.where(d == own + 1, tail, head)
@@ -101,9 +101,9 @@
             values = (row_ref[at], col_ref[at], jnp.int32(1))
             for j, value in enumerate(values):
                 value = jnp.where(live, value, 0).astype(F32)
-                info = jnp.where(lane == rows + 3 * r + j, value, info)
-        out_ref[d, 0:SUBS, :] = jnp.concatenate(parts, axis=0)
-        out_ref[d, SUBS : 2 * SUBS, :] = jnp.where(info_here, info, halo)
+                info = jnp.where(lane == 3 * r + j, value, info)
+        out_ref[pl.ds(PARCEL * d, SUBS), :] = jnp.concatenate(parts, axis=0)
+        out_ref[pl.ds(PARCEL * d + SUBS, PARCEL - SUBS), :] = jnp.where(info_here, info, halo)[0 : PARCEL - SUBS]
         return 0
 
     lax.fori_loop(0, peers, fill, 0, unroll=min(peers, 16))
@@ -173,16 +173,21 @@
     weight, field, design, pairs, gram,
 ):
     own = lax.axis_index("patch")
-    peers = arrived_ref.shape[0]
+    peers = out_ref.shape[0]
     bases = col_taps_ref.shape[0]
     rows = LANES // 2
     last = frame.shape[0] - rows - HEIGHT
     per = VISITS * SUBS
 
-    left = jnp.where(own > 0, arrived_ref[jnp.maximum(own - 1, 0), SUBS : 2 * SUBS, :], 0.0)
-    right = jnp.where(own < peers - 1, arrived_ref[jnp.minimum(own + 1, peers - 1), SUBS : 2 * SUBS, :], 0.0)
-    gap = jnp.zeros((LANES - 4 * SUBS, LANES), F32)
-    halo = jnp.concatenate([pltpu.roll(right, 64, 1), right, gap, pltpu.roll(left, 64, 1), left], axis=0).T
+    skip = PARCEL - SUBS
+    left = arrived_ref[pl.ds(PARCEL * jnp.maximum(own - 1, 0) + skip, SUBS), :]
+    right = arrived_ref[pl.ds(PARCEL * jnp.minimum(own + 1, peers - 1) + skip, SUBS), :]
+    left = jnp.where(own > 0, left, 0.0)
+    right = jnp.where(own < peers - 1, right, 0.0)
+    pick = slice(SUBS - skip, SUBS - 1)
+    ends = [tile[pick] for tile in (pltpu.roll(right, rows, 1), right, left, pltpu.roll(left, rows, 1))]
+    gap = jnp.zeros((LANES - 2 * SHIFT, LANES), F32)
+    halo = jnp.concatenate([ends[0], ends[1], gap, ends[2], ends[3]], axis=0).T
     halo = pltpu.roll(halo, SHIFT, 1)
     starts = iota((rows, LANES), 1) < SHIFT
     first_rows = slice(TOP, TOP + rows)
@@ -213,7 +218,8 @@
     row_taps = row_taps_ref[:, 0:192]
 
     height = LANES // 2 + HEIGHT
-    info = arrived_ref[pl.ds(group * VISITS, VISITS), SUBS + INFO_ROW, :]
+    start = group * (VISITS * PARCEL)
+    info = arrived_ref[pl.ds(start + PARCEL - 1, VISITS, stride=PARCEL), :]
     block = pltpu.roll(info, LANES - 1, 1)
     live = pltpu.roll(info, LANES - 2, 1)
     places = jnp.where(live > 0.0, block * height + info + (TOP - SHIFT), height - 32.0).astype(jnp.int32)
@@ -222,7 +228,7 @@
         terms = []
         masks = []
         for r in range(CAP):
-            first = places[b, LANES // 2 + 3 * r]
+            first = places[b, 3 * r]
             sides = [frame[pl.ds(first + height * side, 32), :] for side in range(2)]
             high, low = split(jnp.concatenate(sides, axis=1))
             terms += [high, low, high]
@@ -252,7 +258,7 @@
         return 0
 
     lax.fori_loop(0, bases, convolve_cols, 0, unroll=bases)
-    science = arrived_ref[pl.ds(group * VISITS, VISITS), 0:SUBS, :].reshape(per, LANES)
+    science = jnp.concatenate([arrived_ref[pl.ds(start + PARCEL * b, SUBS), :] for b in range(VISITS)], axis=0)
     design[PITCH * bases : PITCH * bases + per, :] = jnp.ones((per, LANES), F32)
     design[PITCH * columns : PITCH * columns + per, :] = science
     design[PITCH * (columns + 1) :, :] = jnp.zeros((design.shape[0] - PITCH * (columns + 1), LANES), F32)
@@ -352,7 +358,7 @@
     kept = pltpu.VMEM if peers <= VISITS else jax.ShapeDtypeStruct
     payload, slots = pl.pallas_call(
         pack_kernel,
-        out_shape=(kept((peers, 2 * SUBS, LANES), F32), pltpu.SMEM((strips,), jnp.int32)),
+        out_shape=(kept((peers * PARCEL, LANES), F32), pltpu.SMEM((strips,), jnp.int32)),
         in_specs=[ANY, ANY, ANY, ANY, ANY],
         out_specs=(VMEM, SMEM),
         scratch_shapes=[
@@ -368,7 +374,8 @@
         name="pack",
     )(targets, row_offset, col_block, template, science)
 
-    arrived = lax.all_to_all(payload, "patch", split_axis=0, concat_axis=0, tiled=True)
+    parcels = payload.reshape(peers, 1, PARCEL * LANES)
+    arrived = lax.all_to_all(parcels, "patch", split_axis=0, concat_axis=0, tiled=True).reshape(payload.shape)
 
     frame, col_taps, row_taps, mask = pl.pallas_call(
         prep_kernel,

time: 31.5 us -> 31.3 us (level)
  no operation moved by 1% of the time
where the time goes in v6:
time: 31.3 us; the launch traced here: 31 us
  blocking collectives  9.49 us (30%)
  Pallas kernels  8.49 us (27%)
  starting transfers between devices  7.43 us (24%)
  waiting for transfers between devices  5.52 us (18%)
    all_to_all x1, blocking collectives, on_device(): lax.all_to_all(residual, 'patch', split_axis=0, concat_axis=0, tiled=True)  9.49 us
    all_to_all x1, starting transfers between devices, on_device(): lax.all_to_all(parcels, 'patch', split_axis=0, concat_axis=0, tiled=True)  7.43 us
    all_to_all x1, waiting for transfers between devices, on_device(): lax.all_to_all(parcels, 'patch', split_axis=0, concat_axis=0, tiled=True)  5.52 us
    pallas_call x1, Pallas kernels, on_device(): pl.pallas_call(main_kernel, in_specs=[VMEM, VMEM, VMEM, VMEM, VMEM], out_...  3.97 us
    pallas_call x1, Pallas kernels, on_device(): pl.pallas_call(prep_kernel, out_shape=(pltpu.VMEM(((blocks + 1) * height,...  2.11 us
    pallas_call x1, Pallas kernels, on_device(): pl.pallas_call(pack_kernel, out_shape=(kept((peers * PARCEL, LANES), F32)...  1.7 us
    pallas_call x1, Pallas kernels, on_device(): pl.pallas_call(unpack_kernel, out_shape=jax.ShapeDtypeStruct(science.shap...  0.71 us
  transfers between devices with their start and end apart: 1, of which 1 were waited for; matrix products, arithmetic and copies ran while one was open for 0% of the time, Pallas kernels for 7%

profile of v6, /device:TPU:0, one launch (start us, length us, event | category | flops | bytes accessed | tf_op | source)
XLA Modules:
  0.0 31.0 jit_solution(6872712376106045763)
XLA Ops:
  0.0 1.7 %pack.1 = (f32[224,128]{1,0:T(8,128)}, s32[16]{0:T(128)S(4)}) custom-call(s32[16]{0:T(128)} %bitcast.8, s32[16]{0:T(128)} %row_hbm.1, s32[16]{0:T(128)} %col_hbm.1, f32[64,1024]{1,0:T(8,128)} %template_ref.1, f32[16,4,128]{2,1,0:T(4,128)} %science_hbm.1), custom_call_target="tpu_custom_call" | custom-call | tf_op jit(solution)/shard_map/pack/pallas_call | solution.py:359
  1.7 7.4 %all-to-all-start = ((f32[16,1,1792]{2,1,0:T(1,128)}), f32[16,1,1792]{2,1,0:T(1,128)S(1)}, u32[]{:S(2)}, u32[]{:S(2)}) async-start(f32[16,1,1792]{2,1,0:T(1,128)} %bitcast.1), calls=%async_computation | async-start | bytes 229376 | tf_op jit(solution)/shard_map/all_to_all | solution.py:378
  9.1 2.1 %prep.1 = (f32[936,128]{1,0:T(8,128)S(1)}, bf16[27,256,128]{2,1,0:T(8,128)(2,1)S(1)}, bf16[216,256]{1,0:T(8,128)(2,1)S(1)}, f32[832,128]{1,0:T(8,128)S(1)}) custom-call(f32[64,1024]{1,0:T(8,128)} %template_ref.1, f32[21,27]{1,0:T(8,128)} %bitcast.6, f32[21,27]{1,0:T(8,128)} %bitcast.7, s32[16,24]{1,0:T(8,128)} %stamp_r_ref.1, s32[16,24]{1,0:T(8,128)} %stamp_c_ref.1), custom_call_target="tpu_custom_call" | custom-call | tf_op jit(solution)/shard_map/prep/pallas_call | solution.py:380
  11.3 5.5 %all-to-all-done = f32[16,1,1792]{2,1,0:T(1,128)S(1)} async-done(((f32[16,1,1792]{2,1,0:T(1,128)}), f32[16,1,1792]{2,1,0:T(1,128)S(1)}, u32[]{:S(2)}, u32[]{:S(2)}) %all-to-all-start) | async-done | bytes 114720 | tf_op jit(solution)/shard_map/all_to_all | solution.py:378
  16.8 4.0 %fit.1 = (f32[16,8,128]{2,1,0:T(8,128)S(1)}, f32[936,128]{1,0:T(8,128)S(1)}) custom-call(f32[224,128]{1,0:T(8,128)S(1)} %bitcast.5, f32[936,128]{1,0:T(8,128)S(1)} %get-tuple-element.14.frame_ref, bf16[27,256,128]{2,1,0:T(8,128)(2,1)S(1)} %get-tuple-element.15.col_taps_ref, ...), custom_call_target="tpu_custom_call", output_to_operand_aliasing={{1}: (1, {})} | custom-call | tf_op jit(solution)/shard_map/fit/pallas_call | solution.py:395
  20.7 9.5 %all_to_all.10.back_ref = f32[16,8,128]{2,1,0:T(8,128)S(1)} all-to-all(f32[16,8,128]{2,1,0:T(8,128)S(1)} %get-tuple-element.18), channel_id=1, replica_groups=mesh['groups'=2,'patch'=16] {'patch'}, dimensions={0} | all-to-all | bytes 131072 | tf_op jit(solution)/shard_map/all_to_all | solution.py:412
  30.2 0.7 %unpack.1 = f32[16,4,128]{2,1,0:T(4,128)} custom-call(s32[16]{0:T(128)S(4)} %get-tuple-element.12.slot_ref, f32[16,8,128]{2,1,0:T(8,128)S(1)} %all_to_all.10.back_ref), custom_call_target="tpu_custom_call" | custom-call | tf_op jit(solution)/shard_map/unpack/pallas_call | solution.py:414
Async XLA Ops:
  1.7 15.1 %all-to-all-start = ((f32[16,1,1792]{2,1,0:T(1,128)}), f32[16,1,1792]{2,1,0:T(1,128)S(1)}, u32[]{:S(2)}, u32[]{:S(2)}) async-start(f32[16,1,1792]{2,1,0:T(1,128)} %bitcast.1), calls=%async_computation | async-start | bytes 229376 | tf_op jit(solution)/shard_map/all_to_all | solution.py:378

commit v7 on v6

--- a/solution.py
+++ b/solution.py
@@ -11,7 +11,7 @@
 LANES = 128
 SUBS = 8
 VISITS = 16
-PITCH = VISITS * SUBS + 8
+PITCH = VISITS * SUBS + 1
 
 F32 = jnp.float32
 BF16 = jnp.bfloat16
@@ -110,7 +110,7 @@
 
 
 def prep_kernel(
-    template_ref, rows_ref, cols_ref, stamp_r_ref, stamp_c_ref, frame_ref, col_taps_ref, row_taps_ref, mask_ref, pad_c, pad_t
+    template_ref, rows_ref, cols_ref, stamp_r_ref, stamp_c_ref, frame_ref, col_taps_ref, beyond_ref, row_taps_ref, mask_ref, pad_c, pad_t
 ):
     taps, bases = rows_ref.shape
     own = lax.axis_index("patch")
@@ -158,18 +158,27 @@
         row = jnp.where(lower, row, pltpu.roll(row, 96 - SUBS // CAP, 1))
         tiles.append(row)
     row_taps_ref[...] = jnp.concatenate(tiles, axis=0).astype(BF16)
+    within = iota((LANES, LANES), 1) >= iota((LANES, LANES), 0)
+
     def column(k, _):
         ring = jnp.broadcast_to(pad_c[pl.ds(k, 1), :], (LANES, LANES))
-        high, low = split(pltpu.roll(ring, 0, 1, stride=1, stride_axis=0))
+        ring = pltpu.roll(ring, 0, 1, stride=1, stride_axis=0)
+        high, low = split(jnp.where(within, ring, 0.0))
         col_taps_ref[k, 0:LANES, :] = high
         col_taps_ref[k, LANES : 2 * LANES, :] = low
+        beyond = jnp.where(within, 0.0, ring)[LANES - 32 :]
+        beyond = beyond + pltpu.roll(beyond, 32, 1)
+        beyond = beyond + pltpu.roll(beyond, 64, 1)
+        high, low = split(beyond)
+        beyond_ref[k, 0:32, :] = high
+        beyond_ref[k, 32:64, :] = low
         return 0
 
     lax.fori_loop(0, bases, column, 0, unroll=9)
 
 
 def main_kernel(
-    arrived_ref, frame_ref, col_taps_ref, row_taps_ref, mask_ref, out_ref, frame,
+    arrived_ref, frame_ref, col_taps_ref, beyond_ref, row_taps_ref, mask_ref, out_ref, frame,
     weight, field, design, pairs, gram,
 ):
     own = lax.axis_index("patch")
@@ -197,7 +206,7 @@
 
     def fit_group(group, _):
         fit_visits(
-            group, arrived_ref, col_taps_ref, row_taps_ref, mask_ref, out_ref,
+            group, arrived_ref, col_taps_ref, beyond_ref, row_taps_ref, mask_ref, out_ref,
             frame, weight, field, design, pairs, gram,
         )
         return 0
@@ -209,7 +218,7 @@
 
 
 def fit_visits(
-    group, arrived_ref, col_taps_ref, row_taps_ref, mask_ref, out_ref,
+    group, arrived_ref, col_taps_ref, beyond_ref, row_taps_ref, mask_ref, out_ref,
     frame, weight, field, design, pairs, gram,
 ):
     bases = col_taps_ref.shape[0]
@@ -224,33 +233,51 @@
     live = pltpu.roll(info, LANES - 2, 1)
     places = jnp.where(live > 0.0, block * height + info + (TOP - SHIFT), height - 32.0).astype(jnp.int32)
 
-    for b in range(VISITS):
+    first = [[places[b, 3 * r] for r in range(CAP)] for b in range(VISITS)]
+
+    def tall(windows):
         terms = []
-        masks = []
-        for r in range(CAP):
-            first = places[b, 3 * r]
-            sides = [frame[pl.ds(first + height * side, 32), :] for side in range(2)]
-            high, low = split(jnp.concatenate(sides, axis=1))
+        for window in windows:
+            high, low = split(window)
             terms += [high, low, high]
-            masks.append(mask_ref[pl.ds(first, SUBS), :][0 : SUBS // CAP])
-        at = slice(SUBS * b, SUBS * (b + 1))
-        weight[at, :] = jnp.concatenate(masks, axis=0)
-        across = jnp.dot(row_taps, jnp.concatenate(terms, axis=0), preferred_element_type=F32)
+        return jnp.concatenate(terms, axis=0)
+
+    for b in range(0, VISITS, 2):
+        pair = []
+        for v in (b, b + 1):
+            masks = [mask_ref[pl.ds(at, SUBS), :][0 : SUBS // CAP] for at in first[v]]
+            weight[SUBS * v : SUBS * (v + 1), :] = jnp.concatenate(masks, axis=0)
+            pair.append(tall([frame[pl.ds(at, 32), :] for at in first[v]]))
+        across = jnp.dot(row_taps, jnp.concatenate(pair, axis=1), preferred_element_type=F32)
         for k in range(bases):
-            field[k, at, :] = across[SUBS * k : SUBS * (k + 1)]
-
-    turn = LANES - 32
-    inside = iota((32, LANES), 1) >= iota((32, LANES), 0) + turn
+            rows = across[SUBS * k : SUBS * (k + 1)]
+            field[k, SUBS * b : SUBS * (b + 1), 0:LANES] = rows[:, 0:LANES]
+            field[k, SUBS * (b + 1) : SUBS * (b + 2), 0:LANES] = rows[:, LANES:]
+
+    place_of = iota((32, LANES), 1) // 32
+    for b in range(0, VISITS, 8):
+        sides = []
+        for h in range(b, b + 8, 4):
+            windows = []
+            for r in range(CAP):
+                window = frame[pl.ds(first[h][r] + height, 32), :]
+                for v in range(1, 4):
+                    moved = pltpu.roll(frame[pl.ds(first[h + v][r] + height, 32), :], 32 * v, 1)
+                    window = jnp.where(place_of == v, moved, window)
+                windows.append(window)
+            sides.append(tall(windows))
+        across = jnp.dot(row_taps, jnp.concatenate(sides, axis=1), preferred_element_type=F32)
+        for k in range(bases):
+            for v in range(8):
+                rows = across[SUBS * k : SUBS * (k + 1), LANES * (v // 4) : LANES * (v // 4 + 1)]
+                rows = jnp.where(place_of[0:SUBS] == v % 4, rows, 0.0)
+                field[k, SUBS * (b + v) : SUBS * (b + v + 1), LANES:] = rows
+
+    top = jnp.zeros((LANES - 32, LANES), BF16)
 
     def convolve_cols(k, _):
-        bands = []
-        for term in range(2):
-            ring = col_taps_ref[k, LANES * term : LANES * (term + 1), :]
-            ends = ring[turn:]
-            none = jnp.zeros_like(ends)
-            here = jnp.concatenate([ring[0:turn], jnp.where(inside, ends, none)], axis=0)
-            beyond = jnp.concatenate([jnp.zeros_like(ring[0:turn]), jnp.where(inside, none, ends)], axis=0)
-            bands.append(jnp.concatenate([here, beyond], axis=1))
+        beyond = jnp.concatenate([top, beyond_ref[k, 0:32, :], top, beyond_ref[k, 32:64, :]], axis=0)
+        bands = [jnp.concatenate([col_taps_ref[k], beyond], axis=1)]
         both = jnp.concatenate(split(field[k]), axis=0)
         out = lax.dot_general(both, jnp.concatenate(bands, axis=0), NT, preferred_element_type=F32)
         conv = (out[0:per, LANES:] + out[per:, 0:LANES]) + out[0:per, 0:LANES]
@@ -377,16 +404,17 @@
     parcels = payload.reshape(peers, 1, PARCEL * LANES)
     arrived = lax.all_to_all(parcels, "patch", split_axis=0, concat_axis=0, tiled=True).reshape(payload.shape)
 
-    frame, col_taps, row_taps, mask = pl.pallas_call(
+    frame, col_taps, beyond, row_taps, mask = pl.pallas_call(
         prep_kernel,
         out_shape=(
             pltpu.VMEM(((blocks + 1) * height, LANES), F32),
             pltpu.VMEM((bases, 2 * LANES, LANES), BF16),
+            pltpu.VMEM((bases, 64, LANES), BF16),
             pltpu.VMEM((bases * SUBS, 2 * LANES), BF16),
             pltpu.VMEM((blocks * height, LANES), F32),
         ),
         in_specs=[VMEM, VMEM, VMEM, VMEM, VMEM],
-        out_specs=(VMEM, VMEM, VMEM, VMEM),
+        out_specs=(VMEM, VMEM, VMEM, VMEM, VMEM),
         scratch_shapes=[pltpu.VMEM((32, LANES), F32), pltpu.VMEM((LANES, LANES), F32)],
         name="prep",
     )(template, basis_rows.T, basis_cols.T, stamp_rows, stamp_cols)
@@ -394,7 +422,7 @@
     per = VISITS * SUBS
     residual, _ = pl.pallas_call(
         main_kernel,
-        in_specs=[VMEM, VMEM, VMEM, VMEM, VMEM],
+        in_specs=[VMEM, VMEM, VMEM, VMEM, VMEM, VMEM],
         out_specs=(VMEM, VMEM),
         scratch_shapes=[
             pltpu.VMEM((per, LANES), F32),
@@ -407,7 +435,7 @@
         input_output_aliases={1: 1},
         compiler_params=pltpu.CompilerParams(vmem_limit_bytes=24 << 20),
         name="fit",
-    )(arrived, frame, col_taps, row_taps, mask)
+    )(arrived, frame, col_taps, beyond, row_taps, mask)
 
     returned = lax.all_to_all(residual, "patch", split_axis=0, concat_axis=0, tiled=True)
 

time: 31.3 us -> 31.1 us (level)
  waiting for transfers between devices: 5.52 us -> 4.52 us
  Pallas kernels: 8.49 us -> 9.28 us
    all_to_all x1, waiting for transfers between devices: 5.52 us -> 4.52 us  [on_device(): lax.all_to_all(parcels, 'patch', split_axis=0, concat_axis=0, tiled=True)]
    pallas_call x1, Pallas kernels: 2.11 us -> 3.11 us  [on_device(): pl.pallas_call(prep_kernel, out_shape=(pltpu.VMEM(((blocks + 1) * height,...]
  transfers between devices with their start and end apart: 1 -> 1, of which waited for: 1 -> 1; matrix products, arithmetic and copies ran while one was open for 0% -> 0% of each run, Pallas kernels for 7% -> 10%
where the time goes in v7:
time: 31.1 us; the launch traced here: 30.8 us
  blocking collectives  9.49 us (31%)
  Pallas kernels  9.28 us (30%)
  starting transfers between devices  7.43 us (24%)
  waiting for transfers between devices  4.52 us (15%)
    all_to_all x1, blocking collectives, on_device(): lax.all_to_all(residual, 'patch', split_axis=0, concat_axis=0, tiled=True)  9.49 us
    all_to_all x1, starting transfers between devices, on_device(): lax.all_to_all(parcels, 'patch', split_axis=0, concat_axis=0, tiled=True)  7.43 us
    all_to_all x1, waiting for transfers between devices, on_device(): lax.all_to_all(parcels, 'patch', split_axis=0, concat_axis=0, tiled=True)  4.52 us
    pallas_call x1, Pallas kernels, on_device(): pl.pallas_call(main_kernel, in_specs=[VMEM, VMEM, VMEM, VMEM, VMEM, VMEM]...  3.77 us
    pallas_call x1, Pallas kernels, on_device(): pl.pallas_call(prep_kernel, out_shape=(pltpu.VMEM(((blocks + 1) * height,...  3.11 us
    pallas_call x1, Pallas kernels, on_device(): pl.pallas_call(pack_kernel, out_shape=(kept((peers * PARCEL, LANES), F32)...  1.7 us
    pallas_call x1, Pallas kernels, on_device(): pl.pallas_call(unpack_kernel, out_shape=jax.ShapeDtypeStruct(science.shap...  0.71 us
  transfers between devices with their start and end apart: 1, of which 1 were waited for; matrix products, arithmetic and copies ran while one was open for 0% of the time, Pallas kernels for 10%

profile of v7, /device:TPU:0, one launch (start us, length us, event | category | flops | bytes accessed | tf_op | source)
XLA Modules:
  0.0 30.8 jit_solution(7742195991803244455)
XLA Ops:
  0.0 1.7 %pack.1 = (f32[224,128]{1,0:T(8,128)}, s32[16]{0:T(128)S(4)}) custom-call(s32[16]{0:T(128)} %bitcast.8, s32[16]{0:T(128)} %row_hbm.1, s32[16]{0:T(128)} %col_hbm.1, f32[64,1024]{1,0:T(8,128)} %template_ref.1, f32[16,4,128]{2,1,0:T(4,128)} %science_hbm.1), custom_call_target="tpu_custom_call" | custom-call | tf_op jit(solution)/shard_map/pack/pallas_call | solution.py:386
  1.7 7.4 %all-to-all-start = ((f32[16,1,1792]{2,1,0:T(1,128)}), f32[16,1,1792]{2,1,0:T(1,128)S(1)}, u32[]{:S(2)}, u32[]{:S(2)}) async-start(f32[16,1,1792]{2,1,0:T(1,128)} %bitcast.1), calls=%async_computation | async-start | bytes 229376 | tf_op jit(solution)/shard_map/all_to_all | solution.py:405
  9.1 3.1 %prep.1 = (f32[936,128]{1,0:T(8,128)S(1)}, bf16[27,256,128]{2,1,0:T(8,128)(2,1)S(1)}, bf16[27,64,128]{2,1,0:T(8,128)(2,1)S(1)}, bf16[216,256]{1,0:T(8,128)(2,1)S(1)}, f32[832,128]{1,0:T(8,128)S(1)}) custom-call(f32[64,1024]{1,0:T(8,128)} %template_ref.1, f32[21,27]{1,0:T(8,128)} %bitcast.6, f32[21,27]{1,0:T(8,128)} %bitcast.7, s32[16,24]{1,0:T(8,128)} %stamp_r_ref.1, ...), custom_call_target="tpu_custom_call" | custom-call | tf_op jit(solution)/shard_map/prep/pallas_call | solution.py:407
  12.3 4.5 %all-to-all-done = f32[16,1,1792]{2,1,0:T(1,128)S(1)} async-done(((f32[16,1,1792]{2,1,0:T(1,128)}), f32[16,1,1792]{2,1,0:T(1,128)S(1)}, u32[]{:S(2)}, u32[]{:S(2)}) %all-to-all-start) | async-done | bytes 114720 | tf_op jit(solution)/shard_map/all_to_all | solution.py:405
  16.8 3.8 %fit.1 = (f32[16,8,128]{2,1,0:T(8,128)S(1)}, f32[936,128]{1,0:T(8,128)S(1)}) custom-call(f32[224,128]{1,0:T(8,128)S(1)} %bitcast.5, f32[936,128]{1,0:T(8,128)S(1)} %get-tuple-element.15.frame_ref, bf16[27,256,128]{2,1,0:T(8,128)(2,1)S(1)} %get-tuple-element.16.col_taps_ref, ...), custom_call_target="tpu_custom_call", output_to_operand_aliasing={{1}: (1, {})} | custom-call | tf_op jit(solution)/shard_map/fit/pallas_call | solution.py:423
  20.5 9.5 %all_to_all.10.back_ref = f32[16,8,128]{2,1,0:T(8,128)S(1)} all-to-all(f32[16,8,128]{2,1,0:T(8,128)S(1)} %get-tuple-element.20), channel_id=1, replica_groups=mesh['groups'=2,'patch'=16] {'patch'}, dimensions={0} | all-to-all | bytes 131072 | tf_op jit(solution)/shard_map/all_to_all | solution.py:440
  30.0 0.7 %unpack.1 = f32[16,4,128]{2,1,0:T(4,128)} custom-call(s32[16]{0:T(128)S(4)} %get-tuple-element.13.slot_ref, f32[16,8,128]{2,1,0:T(8,128)S(1)} %all_to_all.10.back_ref), custom_call_target="tpu_custom_call" | custom-call | tf_op jit(solution)/shard_map/unpack/pallas_call | solution.py:442
Async XLA Ops:
  1.7 15.1 %all-to-all-start = ((f32[16,1,1792]{2,1,0:T(1,128)}), f32[16,1,1792]{2,1,0:T(1,128)S(1)}, u32[]{:S(2)}, u32[]{:S(2)}) async-start(f32[16,1,1792]{2,1,0:T(1,128)} %bitcast.1), calls=%async_computation | async-start | bytes 229376 | tf_op jit(solution)/shard_map/all_to_all | solution.py:405

commit v8 on v7

--- a/solution.py
+++ b/solution.py
@@ -142,10 +142,13 @@
         mask_ref[at : at + height, :] = jnp.zeros((height, LANES), F32)
         mask_ref[at + TOP - SHIFT : at + TOP - SHIFT + rows, :] = jnp.minimum(counts[:, LANES * c : LANES * (c + 1)], 1.0)
     pad_t[...] = jnp.zeros_like(pad_t)
-    pad_t[0:taps, 0:bases] = cols_ref[...]
+    for j in range(taps):
+        at = -j % LANES
+        pad_t[at : at + 1, 0:bases] = cols_ref[j : j + 1, :]
     pad_t[32 : 32 + taps, 0:bases] = rows_ref[...]
     filters = pad_t[...].T
-    pad_c[...] = jnp.where(iota((32, LANES), 1) < 32, filters[0:32], 0.0)
+    lane = iota((32, LANES), 1)
+    pad_c[...] = jnp.where((lane == 0) | (lane > LANES - taps), filters[0:32], 0.0)
     full = jnp.where(iota((32, LANES), 1) < 32, pltpu.roll(filters[0:32], LANES - 32, 1), 0.0)
     high = full.astype(BF16).astype(F32)
     base = high + pltpu.roll(high, 32, 1) + pltpu.roll(full - high, 64, 1)
@@ -158,20 +161,17 @@
         row = jnp.where(lower, row, pltpu.roll(row, 96 - SUBS // CAP, 1))
         tiles.append(row)
     row_taps_ref[...] = jnp.concatenate(tiles, axis=0).astype(BF16)
-    within = iota((LANES, LANES), 1) >= iota((LANES, LANES), 0)
+    within = iota((LANES, LANES), 1) <= iota((LANES, LANES), 0)
 
     def column(k, _):
         ring = jnp.broadcast_to(pad_c[pl.ds(k, 1), :], (LANES, LANES))
         ring = pltpu.roll(ring, 0, 1, stride=1, stride_axis=0)
         high, low = split(jnp.where(within, ring, 0.0))
-        col_taps_ref[k, 0:LANES, :] = high
-        col_taps_ref[k, LANES : 2 * LANES, :] = low
-        beyond = jnp.where(within, 0.0, ring)[LANES - 32 :]
-        beyond = beyond + pltpu.roll(beyond, 32, 1)
-        beyond = beyond + pltpu.roll(beyond, 64, 1)
-        high, low = split(beyond)
-        beyond_ref[k, 0:32, :] = high
-        beyond_ref[k, 32:64, :] = low
+        col_taps_ref[k, :, 0:LANES] = high
+        col_taps_ref[k, :, LANES:] = low
+        high, low = split(jnp.where(within, 0.0, ring)[0:32])
+        beyond_ref[k, :, 0:LANES] = high
+        beyond_ref[k, :, LANES:] = low
         return 0
 
     lax.fori_loop(0, bases, column, 0, unroll=9)
@@ -273,18 +273,33 @@
                 rows = jnp.where(place_of[0:SUBS] == v % 4, rows, 0.0)
                 field[k, SUBS * (b + v) : SUBS * (b + v + 1), LANES:] = rows
 
-    top = jnp.zeros((LANES - 32, LANES), BF16)
-
-    def convolve_cols(k, _):
-        beyond = jnp.concatenate([top, beyond_ref[k, 0:32, :], top, beyond_ref[k, 32:64, :]], axis=0)
-        bands = [jnp.concatenate([col_taps_ref[k], beyond], axis=1)]
-        both = jnp.concatenate(split(field[k]), axis=0)
-        out = lax.dot_general(both, jnp.concatenate(bands, axis=0), NT, preferred_element_type=F32)
-        conv = (out[0:per, LANES:] + out[per:, 0:LANES]) + out[0:per, 0:LANES]
-        design[pl.ds(PITCH * k, per), :] = conv
-        return 0
-
-    lax.fori_loop(0, bases, convolve_cols, 0, unroll=bases)
+    none = jnp.zeros((LANES, LANES), BF16)
+
+    def convolve_cols(k):
+        high, low = split(field[k, :, 0:LANES])
+        tail = field[k, :, LANES:]
+        tail_high = tail.astype(BF16).astype(F32)
+        rest = pltpu.roll(tail - tail_high, 32, 1)
+        terms = jnp.concatenate([high, (tail_high + rest).astype(BF16)], axis=1)
+        taps = jnp.concatenate([col_taps_ref[k]] + [beyond_ref[k]] * 4, axis=0)
+        out = jnp.dot(terms, taps, preferred_element_type=F32)
+        return low, out[:, 0:LANES] + out[:, LANES:]
+
+    for k in range(0, bases, 2):
+        low, conv = convolve_cols(k)
+        taps = col_taps_ref[k, :, 0:LANES]
+        if k + 1 == bases:
+            rest = jnp.dot(low, taps, preferred_element_type=F32)
+        else:
+            next_low, next_conv = convolve_cols(k + 1)
+            next_taps = col_taps_ref[k + 1, :, 0:LANES]
+            lows = jnp.concatenate([low, next_low], axis=1)
+            block = jnp.concatenate(
+                [jnp.concatenate([taps, none], axis=1), jnp.concatenate([none, next_taps], axis=1)], axis=0
+            )
+            rest = jnp.dot(lows, block, preferred_element_type=F32)
+            design[PITCH * (k + 1) : PITCH * (k + 1) + per, :] = next_conv + rest[:, LANES:]
+        design[PITCH * k : PITCH * k + per, :] = conv + rest[:, 0:LANES]
     science = jnp.concatenate([arrived_ref[pl.ds(start + PARCEL * b, SUBS), :] for b in range(VISITS)], axis=0)
     design[PITCH * bases : PITCH * bases + per, :] = jnp.ones((per, LANES), F32)
     design[PITCH * columns : PITCH * columns + per, :] = science
@@ -408,8 +423,8 @@
         prep_kernel,
         out_shape=(
             pltpu.VMEM(((blocks + 1) * height, LANES), F32),
-            pltpu.VMEM((bases, 2 * LANES, LANES), BF16),
-            pltpu.VMEM((bases, 64, LANES), BF16),
+            pltpu.VMEM((bases, LANES, 2 * LANES), BF16),
+            pltpu.VMEM((bases, 32, 2 * LANES), BF16),
             pltpu.VMEM((bases * SUBS, 2 * LANES), BF16),
             pltpu.VMEM((blocks * height, LANES), F32),
         ),

time: 31.1 us -> 30.9 us (level)
  Pallas kernels: 9.28 us -> 8.17 us
  waiting for transfers between devices: 4.52 us -> 5.51 us
    pallas_call x1, Pallas kernels: 3.11 us -> 2.12 us  [on_device(): pl.pallas_call(prep_kernel, out_shape=(pltpu.VMEM(((blocks + 1) * height,...]
    all_to_all x1, waiting for transfers between devices: 4.52 us -> 5.51 us  [on_device(): lax.all_to_all(parcels, 'patch', split_axis=0, concat_axis=0, tiled=True)]
  transfers between devices with their start and end apart: 1 -> 1, of which waited for: 1 -> 1; matrix products, arithmetic and copies ran while one was open for 0% -> 0% of each run, Pallas kernels for 10% -> 7%
where the time goes in v8:
time: 30.9 us; the launch traced here: 30.6 us
  blocking collectives  9.49 us (31%)
  Pallas kernels  8.17 us (26%)
  starting transfers between devices  7.43 us (24%)
  waiting for transfers between devices  5.51 us (18%)
    all_to_all x1, blocking collectives, on_device(): lax.all_to_all(residual, 'patch', split_axis=0, concat_axis=0, tiled=True)  9.49 us
    all_to_all x1, starting transfers between devices, on_device(): lax.all_to_all(parcels, 'patch', split_axis=0, concat_axis=0, tiled=True)  7.43 us
    all_to_all x1, waiting for transfers between devices, on_device(): lax.all_to_all(parcels, 'patch', split_axis=0, concat_axis=0, tiled=True)  5.51 us
    pallas_call x1, Pallas kernels, on_device(): pl.pallas_call(main_kernel, in_specs=[VMEM, VMEM, VMEM, VMEM, VMEM, VMEM]...  3.64 us
    pallas_call x1, Pallas kernels, on_device(): pl.pallas_call(prep_kernel, out_shape=(pltpu.VMEM(((blocks + 1) * height,...  2.12 us
    pallas_call x1, Pallas kernels, on_device(): pl.pallas_call(pack_kernel, out_shape=(kept((peers * PARCEL, LANES), F32)...  1.7 us
    pallas_call x1, Pallas kernels, on_device(): pl.pallas_call(unpack_kernel, out_shape=jax.ShapeDtypeStruct(science.shap...  0.71 us
  transfers between devices with their start and end apart: 1, of which 1 were waited for; matrix products, arithmetic and copies ran while one was open for 0% of the time, Pallas kernels for 7%

profile of v8, /device:TPU:0, one launch (start us, length us, event | category | flops | bytes accessed | tf_op | source)
XLA Modules:
  0.0 30.6 jit_solution(1097985155364570347)
XLA Ops:
  0.0 1.7 %pack.1 = (f32[224,128]{1,0:T(8,128)}, s32[16]{0:T(128)S(4)}) custom-call(s32[16]{0:T(128)} %bitcast.8, s32[16]{0:T(128)} %row_hbm.1, s32[16]{0:T(128)} %col_hbm.1, f32[64,1024]{1,0:T(8,128)} %template_ref.1, f32[16,4,128]{2,1,0:T(4,128)} %science_hbm.1), custom_call_target="tpu_custom_call" | custom-call | tf_op jit(solution)/shard_map/pack/pallas_call | solution.py:401
  1.7 7.4 %all-to-all-start = ((f32[16,1,1792]{2,1,0:T(1,128)}), f32[16,1,1792]{2,1,0:T(1,128)S(1)}, u32[]{:S(2)}, u32[]{:S(2)}) async-start(f32[16,1,1792]{2,1,0:T(1,128)} %bitcast.1), calls=%async_computation | async-start | bytes 229376 | tf_op jit(solution)/shard_map/all_to_all | solution.py:420
  9.1 2.1 %prep.1 = (f32[936,128]{1,0:T(8,128)S(1)}, bf16[27,128,256]{2,1,0:T(8,128)(2,1)S(1)}, bf16[27,32,256]{2,1,0:T(8,128)(2,1)S(1)}, bf16[216,256]{1,0:T(8,128)(2,1)S(1)}, f32[832,128]{1,0:T(8,128)S(1)}) custom-call(f32[64,1024]{1,0:T(8,128)} %template_ref.1, f32[21,27]{1,0:T(8,128)} %bitcast.6, f32[21,27]{1,0:T(8,128)} %bitcast.7, s32[16,24]{1,0:T(8,128)} %stamp_r_ref.1, ...), custom_call_target="tpu_custom_call" | custom-call | tf_op jit(solution)/shard_map/prep/pallas_call | solution.py:422
  11.3 5.5 %all-to-all-done = f32[16,1,1792]{2,1,0:T(1,128)S(1)} async-done(((f32[16,1,1792]{2,1,0:T(1,128)}), f32[16,1,1792]{2,1,0:T(1,128)S(1)}, u32[]{:S(2)}, u32[]{:S(2)}) %all-to-all-start) | async-done | bytes 114720 | tf_op jit(solution)/shard_map/all_to_all | solution.py:420
  16.8 3.6 %fit.1 = (f32[16,8,128]{2,1,0:T(8,128)S(1)}, f32[936,128]{1,0:T(8,128)S(1)}) custom-call(f32[224,128]{1,0:T(8,128)S(1)} %bitcast.5, f32[936,128]{1,0:T(8,128)S(1)} %get-tuple-element.15.frame_ref, bf16[27,128,256]{2,1,0:T(8,128)(2,1)S(1)} %get-tuple-element.16.col_taps_ref, ...), custom_call_target="tpu_custom_call", output_to_operand_aliasing={{1}: (1, {})} | custom-call | tf_op jit(solution)/shard_map/fit/pallas_call | solution.py:438
  20.4 9.5 %all_to_all.10.back_ref = f32[16,8,128]{2,1,0:T(8,128)S(1)} all-to-all(f32[16,8,128]{2,1,0:T(8,128)S(1)} %get-tuple-element.20), channel_id=1, replica_groups=mesh['groups'=2,'patch'=16] {'patch'}, dimensions={0} | all-to-all | bytes 131072 | tf_op jit(solution)/shard_map/all_to_all | solution.py:455
  29.9 0.7 %unpack.1 = f32[16,4,128]{2,1,0:T(4,128)} custom-call(s32[16]{0:T(128)S(4)} %get-tuple-element.13.slot_ref, f32[16,8,128]{2,1,0:T(8,128)S(1)} %all_to_all.10.back_ref), custom_call_target="tpu_custom_call" | custom-call | tf_op jit(solution)/shard_map/unpack/pallas_call | solution.py:457
Async XLA Ops:
  1.7 15.1 %all-to-all-start = ((f32[16,1,1792]{2,1,0:T(1,128)}), f32[16,1,1792]{2,1,0:T(1,128)S(1)}, u32[]{:S(2)}, u32[]{:S(2)}) async-start(f32[16,1,1792]{2,1,0:T(1,128)} %bitcast.1), calls=%async_computation | async-start | bytes 229376 | tf_op jit(solution)/shard_map/all_to_all | solution.py:420
